TPU v7x, 256 devices: a whole 4x4x8 slice. The times are simulated.
256 devices in a mesh: ctx: 32 (over x, z), head: 8 (over y, core).
Axes of the slice: x: 4, y: 4, z: 8, core: 2. Of those that a mesh axis runs over, the one named last changes fastest.
Arguments:
- queries: bfloat16 [65536, 128], P(('ctx', 'head')), may hold values from -6 to 6
- keys: bfloat16 [65536, 128], P(('ctx', 'head')), may hold values from -0.03125 to 0.03125
- values: bfloat16 [65536, 4096], P('ctx', 'head'), may hold values from -6 to 6
- tier_weight_rows: int32 [10, 65536], P(None, 'ctx'), may hold values from 0 to 15
- level_table: float32 [16, 32], P(None, 'head'), may hold values from 0.1 to 10
Outputs:
- mixed: bfloat16 [65536, 4096], P('ctx', 'head')
All inputs are finite; a program needn't handle non-finite values.
Results may differ from a plain program's by a relative error of at most 0.0049.
Values may be sent and summed in bfloat16 or wider, within the bound.
A program may use at most 192 MiB of HBM per device.

v0:
```python
import jax
import jax.numpy as jnp
from jax import lax
from jax.sharding import Mesh
from jax.sharding import PartitionSpec as P

GROUP = 128
HEAD = ("head_0", "head_1")
CTX_HEAD = ("ctx", "head_0", "head_1")


def laid_out(parts, dim):
    lengths = list(parts.shape[1:])
    lengths[dim] *= parts.shape[0]
    return jnp.moveaxis(parts, 0, dim).reshape(lengths)


def all_blocks(x, axes, order):
    parts = x
    for k in order:
        parts = lax.all_gather(parts, axes[k])
    done = order[::-1]
    back = [done.index(k) for k in range(len(axes))]
    parts = parts.transpose(*back, *range(len(axes), parts.ndim))
    return parts.reshape(-1, *x.shape)


def gathered_by_axis(x, axes, order, dim):
    return laid_out(all_blocks(x, axes, order), dim)


def swapped(value, axis, distance):
    mask = 2**distance
    pairs = [(source, source ^ mask) for source in range(lax.axis_size(axis))]
    return lax.ppermute(value, axis, pairs)


def local(queries, keys, values, tier_weight_rows, level_table):
    q_whole, k_whole = (
        gathered_by_axis(queries, HEAD, (0, 1), 0),
        gathered_by_axis(keys, HEAD, (0, 1), 0),
    )
    tok_rows = values.shape[0]
    columns = values.shape[1]
    head_count = level_table.shape[1]
    head_width = columns // head_count
    key_width = q_whole.shape[1]
    local_bits = (tok_rows // GROUP).bit_length() - 1
    context_exponent = lax.axis_size("ctx").bit_length() - 1
    classes = jnp.arange(level_table.shape[0], dtype=jnp.int32)
    onehot = (tier_weight_rows[:, :, None] == classes[None, None, :]).astype(jnp.float32)
    weights = jnp.einsum("ltc,ch->lth", onehot, level_table, precision=lax.Precision.HIGHEST)
    share = weights / jnp.sum(weights, axis=0)
    local_state = lax.dot_general(
        k_whole, values, (((0,), (0,)), ((), ())), preferred_element_type=jnp.float32
    )
    me_index = lax.axis_index("ctx")
    subtree = local_state
    sibling_states = []
    for bit in range(context_exponent):
        incoming_partner_sums = swapped(subtree, "ctx", bit)
        mine_bit = me_index >> bit & 1
        sibling_states.append(
            jnp.where(mine_bit == 1, incoming_partner_sums, jnp.zeros_like(incoming_partner_sums))
        )
        subtree = subtree + incoming_partner_sums

    def weigh(part, level):
        scaled = part.reshape(tok_rows, head_count, head_width) * share[level][:, :, None]
        return scaled.reshape(tok_rows, columns)

    groups = tok_rows // GROUP
    q_groups = q_whole.reshape(groups, GROUP, key_width)
    k_groups = k_whole.reshape(groups, GROUP, key_width)
    scores = jnp.einsum("nik,njk->nij", q_groups, k_groups, preferred_element_type=jnp.float32)
    causal = jnp.tril(jnp.ones((GROUP, GROUP), dtype=bool))
    scores = jnp.where(causal[None], scores, 0.0).astype(jnp.bfloat16)
    near = jnp.einsum(
        "nij,njc->nic",
        scores,
        values.reshape(groups, GROUP, columns),
        preferred_element_type=jnp.float32,
    )
    total = weigh(near.reshape(tok_rows, columns), 0)
    for level in range(1, local_bits + 1):
        half = GROUP * 2 ** (level - 1)
        blocks = tok_rows // (2 * half)
        grouped_probe_matrix = k_whole.reshape(blocks, 2, half, key_width)
        grouped_content_matrix = values.reshape(blocks, 2, half, columns)
        query_blocked = q_whole.reshape(blocks, 2, half, key_width)
        cumulative_memory = jnp.einsum(
            "bsk,bsc->bkc",
            grouped_probe_matrix[:, 0],
            grouped_content_matrix[:, 0],
            preferred_element_type=jnp.float32,
        )
        cumulative_memory = cumulative_memory.astype(jnp.bfloat16)
        upper_half_branch = jnp.einsum(
            "bsk,bkc->bsc",
            query_blocked[:, 1],
            cumulative_memory,
            preferred_element_type=jnp.float32,
        )
        part = jnp.stack([jnp.zeros_like(upper_half_branch), upper_half_branch], axis=1).reshape(
            tok_rows, columns
        )
        total = total + weigh(part, level)
    for bit in range(context_exponent):
        cumulative_memory = sibling_states[bit].astype(jnp.bfloat16)
        part = jnp.dot(q_whole, cumulative_memory, preferred_element_type=jnp.float32)
        total = total + weigh(part, 1 + local_bits + bit)
    return total.astype(jnp.bfloat16)


def solution(mesh):
    torus = Mesh(mesh.devices.reshape(mesh.shape["ctx"], 4, 2), ("ctx", "head_0", "head_1"))
    return jax.shard_map(
        local,
        mesh=torus,
        in_specs=(
            P(CTX_HEAD, None),
            P(CTX_HEAD, None),
            P("ctx", HEAD),
            P(None, "ctx"),
            P(None, HEAD),
        ),
        out_specs=P("ctx", HEAD),
        check_vma=False,
    )
```

profile of v0, /device:TPU:6, one launch (start us, length us, event | category | flops | bytes accessed | tf_op | source)
XLA Modules:
  0.0 160.0 jit_solution(13274150016404325897)
XLA Ops:
  0.0 13.1 %all-gather.2 = bf16[1024,128]{1,0:T(8,128)(2,1)S(1)} all-gather(bf16[256,128]{1,0:T(8,128)(2,1)} %param.6), channel_id=4, replica_groups=mesh['ctx'=32,'head_0'=4,'head_1'=2] {'head_0'}, dimensions={0}, use_global_device_ids=true | all-gather | bytes 327680 | tf_op jit(solution)/shard_map/all_gather | solution.py:21
  13.1 2.2 %all-gather.3 = bf16[8,256,128]{2,1,0:T(8,128)(2,1)S(1)} all-gather(bf16[4,256,128]{2,1,0:T(8,128)(2,1)S(1)} %bitcast.248), channel_id=5, replica_groups=mesh['ctx'=32,'head_0'=4,'head_1'=2] {'head_1'}, dimensions={0}, use_global_device_ids=true | all-gather | bytes 786432 | tf_op jit(solution)/shard_map/all_gather | solution.py:21
  15.3 3.0 %fusion.38 = f32[128,512]{1,0:T(8,128)} fusion(bf16[2048,128]{1,0:T(8,128)(2,1)S(1)} %bitcast.236, bf16[2048,512]{1,0:T(8,128)(2,1)} %param.7), kind=kOutput, calls=%fused_computation.87 | convolution fusion | flops 268435456 | bytes 2883584 | tf_op jit(solution)/shard_map/dot_general | solution.py:54
  20.3 12.3 %all-gather = bf16[1024,128]{1,0:T(8,128)(2,1)S(1)} all-gather(bf16[256,128]{1,0:T(8,128)(2,1)S(1)} %copy-done.5), channel_id=2, replica_groups=mesh['ctx'=32,'head_0'=4,'head_1'=2] {'head_0'}, dimensions={0}, use_global_device_ids=true | all-gather | bytes 327680 | tf_op jit(solution)/shard_map/all_gather | solution.py:21
  32.5 2.2 %all-gather.1 = bf16[8,256,128]{2,1,0:T(8,128)(2,1)S(1)} all-gather(bf16[4,256,128]{2,1,0:T(8,128)(2,1)S(1)} %bitcast.249), channel_id=3, replica_groups=mesh['ctx'=32,'head_0'=4,'head_1'=2] {'head_1'}, dimensions={0}, use_global_device_ids=true | all-gather | bytes 786432 | tf_op jit(solution)/shard_map/all_gather | solution.py:21
  35.5 2.0 %copy.79 = bf16[2,4,256,128]{2,3,1,0:T(8,128)(2,1)} copy(bf16[2,4,256,128]{3,2,1,0:T(8,128)(2,1)} %bitcast.242) | data formatting | bytes 1048576 | tf_op jit(solution)/shard_map/all_gather | solution.py:21
  37.6 3.0 %convolution_bitcast_fusion = f32[4,1,256,512]{3,2,1,0:T(8,128)} fusion(bf16[4,2,256,512]{3,2,1,0:T(8,128)(2,1)S(1)} %bitcast.226, bf16[4,2,256,128]{2,3,0,1:T(8,128)(2,1)} %bitcast.247, bf16[4,2,256,128]{3,2,0,1:T(8,128)(2,1)} %bitcast.244), kind=kOutput, calls=%fused_computation.20 | convolution fusion | flops 268697600 | bytes 3670016 | tf_op jit(solution)/shard_map/bsk,bkc->bsc/dot_general | solution.py:98
  40.5 4.1 %stack.27.clone = f32[4,2,256,512]{3,2,1,0:T(8,128)} pad(f32[4,1,256,512]{3,2,1,0:T(8,128)} %convolution_bitcast_fusion, f32[]{:T(128)} %constant.8.clone.1), padding=0_0x1_0x0_0x0_0 | pad | bytes 6291460 | tf_op jit(solution)/shard_map/stack | solution.py:104
  44.6 5.4 %copy.91 = f32[2048,512]{0,1:T(8,128)} copy(f32[2048,512]{1,0:T(8,128)} %bitcast.233) | data formatting | bytes 8388608 | tf_op jit(solution)/shard_map/reshape;reshape | solution.py:69
  50.0 2.1 %convolution_bitcast_fusion.1 = f32[8,1,128,512]{3,2,1,0:T(8,128)} fusion(bf16[8,2,128,512]{3,2,1,0:T(8,128)(2,1)S(1)} %bitcast.227, bf16[8,2,128,128]{3,2,1,0:T(8,128)(2,1)S(1)} %bitcast.237, bf16[8,2,128,128]{3,2,1,0:T(8,128)(2,1)S(1)} %bitcast.217), kind=kOutput, calls=%fused_computation.21 | convolution fusion | flops 268959744 | bytes 3670016 | tf_op jit(solution)/shard_map/bsk,bkc->bsc/dot_general | solution.py:98
  52.1 4.1 %stack.25.clone = f32[8,2,128,512]{3,2,1,0:T(8,128)} pad(f32[8,1,128,512]{3,2,1,0:T(8,128)} %convolution_bitcast_fusion.1, f32[]{:T(128)} %constant.8.clone.1), padding=0_0x1_0x0_0x0_0 | pad | bytes 6291460 | tf_op jit(solution)/shard_map/stack | solution.py:104
  56.1 5.4 %copy.88 = f32[2048,512]{0,1:T(8,128)} copy(f32[2048,512]{1,0:T(8,128)} %bitcast.234) | data formatting | bytes 8388608 | tf_op jit(solution)/shard_map/reshape;reshape | solution.py:69
  61.6 2.0 %convolution_bitcast_fusion.2 = f32[2,1,512,512]{3,2,1,0:T(8,128)} fusion(bf16[2,2,512,512]{3,2,1,0:T(8,128)(2,1)S(1)} %bitcast.228, bf16[2,2,512,128]{3,2,1,0:T(8,128)(2,1)S(1)} %bitcast.238, bf16[2,2,512,128]{3,2,1,0:T(8,128)(2,1)S(1)} %bitcast.218), kind=kOutput, calls=%fused_computation.22 | convolution fusion | flops 268566528 | bytes 3670016 | tf_op jit(solution)/shard_map/bsk,bkc->bsc/dot_general | solution.py:98
  63.6 4.0 %stack.29.clone = f32[2,2,512,512]{3,2,1,0:T(8,128)} pad(f32[2,1,512,512]{3,2,1,0:T(8,128)} %convolution_bitcast_fusion.2, f32[]{:T(128)} %constant.8.clone.1), padding=0_0x1_0x0_0x0_0 | pad | bytes 6291460 | tf_op jit(solution)/shard_map/stack | solution.py:104
  67.6 5.4 %copy.98 = f32[2048,512]{0,1:T(8,128)} copy(f32[2048,512]{1,0:T(8,128)} %bitcast.235) | data formatting | bytes 8388608 | tf_op jit(solution)/shard_map/reshape;reshape | solution.py:69
  72.9 2.1 %convolution_bitcast_fusion.3 = f32[1,1,1024,512]{2,3,1,0:T(8,128)} fusion(bf16[1,2,1024,512]{3,2,1,0:T(8,128)(2,1)S(1)} %bitcast.229, bf16[1,2,1024,128]{3,2,1,0:T(8,128)(2,1)S(1)} %bitcast.219, bf16[1,2,1024,128]{3,2,1,0:T(8,128)(2,1)S(1)} %bitcast.239), kind=kOutput, calls=%fused_computation.23 | convolution fusion | flops 268500992 | bytes 3670016 | tf_op jit(solution)/shard_map/bsk,bkc->bsc/dot_general | solution.py:98
  75.0 2.9 %copy.121 = f32[1,1,1024,512]{3,2,1,0:T(8,128)} copy(f32[1,1,1024,512]{2,3,1,0:T(8,128)} %convolution_bitcast_fusion.3) | data formatting | bytes 4194304
  77.9 4.0 %stack.31.clone = f32[1,2,1024,512]{3,2,1,0:T(8,128)} pad(f32[1,1,1024,512]{3,2,1,0:T(8,128)} %copy.121, f32[]{:T(128)} %constant.8.clone.1), padding=0_0x1_0x0_0x0_0 | pad | bytes 6291460 | tf_op jit(solution)/shard_map/stack | solution.py:104
  82.0 5.4 %copy.102 = f32[2048,512]{0,1:T(8,128)} copy(f32[2048,512]{1,0:T(8,128)} %bitcast.232) | data formatting | bytes 8388608 | tf_op jit(solution)/shard_map/reshape;reshape | solution.py:69
  87.3 3.0 %fusion.12 = f32[16,128,512]{2,1,0:T(8,128)} fusion(bf16[16,128,512]{2,1,0:T(8,128)(2,1)S(1)} %bitcast.230, bf16[16,128,128]{2,1,0:T(8,128)(2,1)S(1)} %bitcast.220, bf16[16,128,128]{2,1,0:T(8,128)(2,1)S(1)} %bitcast.240, pred[128,128]{1,0:T(8,128)(4,1)S(1)} %iota_compare_fusion.2), kind=kOutput, calls=%fused_computation.30 | convolution fusion | flops 336068608 | bytes 7356416 | tf_op jit(solution)/shard_map/nij,njc->nic/dot_general | solution.py:78
  90.3 5.4 %copy.81 = f32[2048,512]{0,1:T(8,128)} copy(f32[2048,512]{1,0:T(8,128)} %bitcast.231) | data formatting | bytes 8388608 | tf_op jit(solution)/shard_map/reshape;reshape | solution.py:69
  97.4 3.4 %collective-permute-start.1 = (f32[128,512]{1,0:T(8,128)S(1)}, f32[128,512]{1,0:T(8,128)S(1)}, u32[]{:S(2)}, u32[]{:S(2)}) collective-permute-start(f32[128,512]{1,0:T(8,128)S(1)} %add.52), channel_id=1, source_target_pairs={{0,16},{8,24},{16,0},{24,8},{32,48},{40,56},{48,32},{56,40},{64,80... | collective-permute-start | bytes 786440 | tf_op jit(solution)/shard_map/ppermute | solution.py:35
  101.5 11.0 %collective-permute-done.1 = f32[128,512]{1,0:T(8,128)S(1)} collective-permute-done((f32[128,512]{1,0:T(8,128)S(1)}, f32[128,512]{1,0:T(8,128)S(1)}, u32[]{:S(2)}, u32[]{:S(2)}) %collective-permute-start.1) | collective-permute-done | bytes 262176 | tf_op jit(solution)/shard_map/ppermute | solution.py:35
  112.5 6.2 %collective-permute-start.2 = (f32[128,512]{1,0:T(8,128)S(1)}, f32[128,512]{1,0:T(8,128)S(1)}, u32[]{:S(2)}, u32[]{:S(2)}) collective-permute-start(f32[128,512]{1,0:T(8,128)S(1)} %add.54), channel_id=1, source_target_pairs={{0,32},{8,40},{16,48},{24,56},{32,0},{40,8},{48,16},{56,24},{64,96... | collective-permute-start | bytes 786440 | tf_op jit(solution)/shard_map/ppermute | solution.py:35
  118.8 2.7 %fusion.17 = f32[512,2048]{1,0:T(8,128)} fusion(bf16[2048,128]{1,0:T(8,128)(2,1)S(1)} %bitcast.222, f32[128,512]{1,0:T(8,128)S(1)} %collective-permute-done.1, pred[]{:T(512)S(6)} %eq.32), kind=kOutput, calls=%fused_computation.55 | convolution fusion | flops 268500992 | bytes 4980737 | tf_op jit(solution)/shard_map/dot_general | solution.py:110
  121.5 9.1 %collective-permute-done.2 = f32[128,512]{1,0:T(8,128)S(1)} collective-permute-done((f32[128,512]{1,0:T(8,128)S(1)}, f32[128,512]{1,0:T(8,128)S(1)}, u32[]{:S(2)}, u32[]{:S(2)}) %collective-permute-start.2) | collective-permute-done | bytes 262176 | tf_op jit(solution)/shard_map/ppermute | solution.py:35
  131.7 2.7 %fusion.18 = f32[512,2048]{1,0:T(8,128)} fusion(bf16[2048,128]{1,0:T(8,128)(2,1)S(1)} %bitcast.223, f32[128,512]{1,0:T(8,128)S(1)} %collective-permute-done.2, pred[]{:T(512)S(6)} %eq.33), kind=kOutput, calls=%fused_computation.56 | convolution fusion | flops 268500992 | bytes 4980737 | tf_op jit(solution)/shard_map/dot_general | solution.py:110
  134.4 3.9 %collective-permute-done.3 = f32[128,512]{1,0:T(8,128)S(1)} collective-permute-done((f32[128,512]{1,0:T(8,128)S(1)}, f32[128,512]{1,0:T(8,128)S(1)}, u32[]{:S(2)}, u32[]{:S(2)}) %collective-permute-start.3) | collective-permute-done | bytes 262176 | tf_op jit(solution)/shard_map/ppermute | solution.py:35
  139.4 2.7 %fusion.19 = f32[512,2048]{1,0:T(8,128)} fusion(bf16[2048,128]{1,0:T(8,128)(2,1)S(1)} %bitcast.224, f32[128,512]{1,0:T(8,128)S(1)} %collective-permute-done.3, pred[]{:T(512)S(6)} %eq.34), kind=kOutput, calls=%fused_computation.57 | convolution fusion | flops 268500992 | bytes 4980737 | tf_op jit(solution)/shard_map/dot_general | solution.py:110
  142.1 2.8 %collective-permute-done.4 = bf16[128,512]{1,0:T(8,128)(2,1)S(1)} collective-permute-done((bf16[128,512]{1,0:T(8,128)(2,1)S(1)}, bf16[128,512]{1,0:T(8,128)(2,1)S(1)}, u32[]{:S(2)}, u32[]{:S(2)}) %collective-permute-start.4) | collective-permute-done | bytes 131104 | tf_op jit(solution)/shard_map/ppermute | solution.py:35
  144.9 12.6 %fusion.1 = bf16[2048,512]{0,1:T(8,128)(2,1)S(1)} fusion(f32[512,2048]{1,0:T(8,128)} %fusion.19, f32[512,2048]{1,0:T(8,128)} %fusion.18, f32[512,2048]{1,0:T(8,128)} %fusion.17, f32[512,2048]{1,0:T(8,128)S(1)} %fusion.16, f32[2048,512]{0,1:T(8,128)} %copy.102, f32[2048,512]{0,1:T(8,128)} %copy.98, f32[2048,512]{0,1:T(8,128)} %copy.91, ...), kind=kOutput, calls=%fused_computation.2 | convolution fusion | flops 289472512 | bytes 40828928 | tf_op jit(solution)/shard_map/dot_general | solution.py:110
  157.5 2.5 %copy.105 = bf16[2048,512]{1,0:T(8,128)(2,1)} copy(bf16[2048,512]{0,1:T(8,128)(2,1)S(1)} %fusion.1) | data formatting | bytes 4194304 | tf_op jit(solution)/shard_map/convert_element_type | solution.py:112
  (28 shorter events, 7.4 us)
Async XLA Ops:
  0.0 95.7 %copy-start = (f32[16,4]{0,1:T(4,128)S(1)}, f32[16,4]{0,1:T(4,128)}, u32[]{:S(2)}) copy-start(f32[16,4]{0,1:T(4,128)} %param.9) | copy-start | bytes 772
  0.0 37.6 %copy-start.1 = (bf16[2048,512]{1,0:T(8,128)(2,1)S(1)}, bf16[2048,512]{1,0:T(8,128)(2,1)}, u32[]{:S(2)}) copy-start(bf16[2048,512]{1,0:T(8,128)(2,1)} %param.7) | copy-start | bytes 6291460
  0.0 20.3 %copy-start.5 = (bf16[256,128]{1,0:T(8,128)(2,1)S(1)}, bf16[256,128]{1,0:T(8,128)(2,1)}, u32[]{:S(2)}) copy-start(bf16[256,128]{1,0:T(8,128)(2,1)} %param.5) | copy-start | bytes 196612
  15.3 19.4 %copy-start.2 = (bf16[8,256,128]{2,1,0:T(8,128)(2,1)}, bf16[8,256,128]{2,1,0:T(8,128)(2,1)S(1)}, u32[]{:S(2)}) copy-start(bf16[8,256,128]{2,1,0:T(8,128)(2,1)S(1)} %all-gather.3) | copy-start | bytes 1572868
  18.3 78.0 %collective-permute-start = (f32[128,512]{1,0:T(8,128)}, f32[128,512]{1,0:T(8,128)S(1)}, u32[]{:S(2)}, u32[]{:S(2)}) collective-permute-start(f32[128,512]{1,0:T(8,128)} %fusion.38), channel_id=1, source_target_pairs={{0,8},{8,0},{16,24},{24,16},{32,40},{40,32},{48,56},{56,48},{64,72... | collective-permute-start | bytes 786440 | tf_op jit(solution)/shard_map/ppermute | solution.py:35
  34.7 0.8 copy-start.3
  90.3 5.4 %copy-start.4 = (s32[10,2048]{1,0:T(8,128)S(1)}, s32[10,2048]{1,0:T(8,128)}, u32[]{:S(2)}) copy-start(s32[10,2048]{1,0:T(8,128)} %param.8) | copy-start | bytes 245764
  97.4 15.1 %collective-permute-start.1 = (f32[128,512]{1,0:T(8,128)S(1)}, f32[128,512]{1,0:T(8,128)S(1)}, u32[]{:S(2)}, u32[]{:S(2)}) collective-permute-start(f32[128,512]{1,0:T(8,128)S(1)} %add.52), channel_id=1, source_target_pairs={{0,16},{8,24},{16,0},{24,8},{32,48},{40,56},{48,32},{56,40},{64,80... | collective-permute-start | bytes 786440 | tf_op jit(solution)/shard_map/ppermute | solution.py:35
  112.5 18.0 %collective-permute-start.2 = (f32[128,512]{1,0:T(8,128)S(1)}, f32[128,512]{1,0:T(8,128)S(1)}, u32[]{:S(2)}, u32[]{:S(2)}) collective-permute-start(f32[128,512]{1,0:T(8,128)S(1)} %add.54), channel_id=1, source_target_pairs={{0,32},{8,40},{16,48},{24,56},{32,0},{40,8},{48,16},{56,24},{64,96... | collective-permute-start | bytes 786440 | tf_op jit(solution)/shard_map/ppermute | solution.py:35
  130.6 7.8 %collective-permute-start.3 = (f32[128,512]{1,0:T(8,128)S(1)}, f32[128,512]{1,0:T(8,128)S(1)}, u32[]{:S(2)}, u32[]{:S(2)}) collective-permute-start(f32[128,512]{1,0:T(8,128)S(1)} %add.56), channel_id=1, source_target_pairs={{0,64},{8,72},{16,80},{24,88},{32,96},{40,104},{48,112},{56,120},{... | collective-permute-start | bytes 786440 | tf_op jit(solution)/shard_map/ppermute | solution.py:35
  138.4 6.6 %collective-permute-start.4 = (bf16[128,512]{1,0:T(8,128)(2,1)S(1)}, bf16[128,512]{1,0:T(8,128)(2,1)S(1)}, u32[]{:S(2)}, u32[]{:S(2)}) collective-permute-start(bf16[128,512]{1,0:T(8,128)(2,1)S(1)} %add.58), channel_id=1, source_target_pairs={{0,128},{8,136},{16,144},{24,152},{32,160},{40,168},{48,176},{56,1... | collective-permute-start | bytes 393224 | tf_op jit(solution)/shard_map/ppermute | solution.py:35
where the time goes:
time: 161 us; the launch traced here: 160 us
  local copies, waits for them, and re-layouts  51.5 us (32%)
  matrix products  37.1 us (23%)
  blocking collectives  29.7 us (18%)
  waiting for transfers between devices  26.8 us (17%)
  starting transfers between devices  13.7 us (9%)
    all_gather x4, blocking collectives, all_blocks(): parts = lax.all_gather(parts, axes[k])  29.7 us
    another operation x5, local copies, waits for them, and re-layouts, weigh(): part.reshape(tok_rows, head_count, head_width) * share[level][:, :, None]  26.9 us
    ppermute x5, waiting for transfers between devices, swapped(): return lax.ppermute(value, axis, pairs)  26.8 us
    dot_general x5, matrix products, local(): jnp.dot(q_whole, cumulative_memory, preferred_element_type=jnp.float32)  21.4 us
    another operation x4, local copies, waits for them, and re-layouts, local(): jnp.stack([jnp.zeros_like(upper_half_branch), upper_half_branch], axis=1)  16.2 us
    ppermute x5, starting transfers between devices, swapped(): return lax.ppermute(value, axis, pairs)  13.7 us
    dot_general x4, matrix products, local(): jnp.einsum('bsk,bkc->bsc', query_blocked[:, 1], cumulative_memory, prefer...  9.13 us
    unnamed x14, local copies, waits for them, and re-layouts  3.7 us
  transfers between devices with their start and end apart: 5, of which 4 were waited for; matrix products, arithmetic and copies ran while one was open for 44% of the time, Pallas kernels for 0%

commit v1 on v0

v1 whole, which is shorter than its diff:
```python
import functools

import jax
import jax.numpy as jnp
from jax import lax
from jax.experimental import pallas as pl
from jax.experimental.pallas import tpu as pltpu
from jax.sharding import PartitionSpec as P

GROUP = 128
X, Y, Z = 4, 4, 8
CHUNK = 16
F32, BF16 = jnp.float32, jnp.bfloat16
DMA = pltpu.SemaphoreType.DMA


def nt(a, b):
    return lax.dot_general(a, b, (((1,), (1,)), ((), ())), preferred_element_type=F32)


def tn(a, b):
    return lax.dot_general(a, b, (((0,), (0,)), ((), ())), preferred_element_type=F32)


def nn(a, b):
    return jnp.dot(a, b, preferred_element_type=F32)


def kernel(
    q_in, k_in, v_in, rows_in, table_in, out,
    qbuf, kbuf, vbuf, rows, table, sh_t, sh, total, pairs, lev1, lev2, lev3, lev4,
    send, recv, pair6, half7, row_t, row_r, zst, xst, qs, obuf,
    loc_sem, v_sem, o_sem, gs_sem, gr_sem, as_sem, ar_sem, zs_sem, zr_sem,
    xs_sem, xr_sem, bs_sem, br_sem,
):
    ctx = lax.axis_index("ctx")
    head = lax.axis_index("head")
    x, z = ctx // Z, ctx % Z
    y, c = head // 2, head % 2
    sib = y * 2 + 1 - c
    up = ((y + 1) % Y) * 2 + c
    down = ((y + 3) % Y) * 2 + c
    far = ((y + 2) % Y) * 2 + c
    up_s, down_s, far_s = (((y + d) % Y) * 2 + 1 - c for d in (1, 3, 2))

    def remote(src, dst, ss, rs, ctx_to=ctx, head_to=head):
        return pltpu.make_async_remote_copy(
            src, dst, ss, rs, device_id=(ctx_to, head_to), device_id_type=pl.DeviceIdType.MESH
        )

    def z_at(d):
        return (z + d) % Z

    def ctx_z(d):
        return x * Z + z_at(d)

    copies = [
        pltpu.make_async_copy(rows_in, rows, loc_sem.at[0]),
        pltpu.make_async_copy(table_in, table, loc_sem.at[1]),
        pltpu.make_async_copy(k_in, kbuf.at[pl.ds(2 * head, 2)], loc_sem.at[2]),
        pltpu.make_async_copy(q_in, qbuf.at[pl.ds(2 * head, 2)], loc_sem.at[3]),
    ]
    for cp in copies:
        cp.start()
    v_copies = [
        pltpu.make_async_copy(v_in.at[pl.ds(2 * i, 2)], vbuf.at[pl.ds(2 * i, 2)], v_sem.at[i])
        for i in range(8)
    ]
    for cp in v_copies:
        cp.start()

    barrier = pltpu.get_barrier_semaphore()
    for d in range(1, 8):
        pl.semaphore_signal(
            barrier, 1, device_id=(ctx, (head + d) % 8), device_id_type=pl.DeviceIdType.MESH
        )
    for d in range(1, Z):
        pl.semaphore_signal(
            barrier, 1, device_id=(ctx_z(d), head), device_id_type=pl.DeviceIdType.MESH
        )
    for d in range(1, X):
        pl.semaphore_signal(
            barrier, 1, device_id=((x + d) % X * Z + z, head), device_id_type=pl.DeviceIdType.MESH
        )
    pl.semaphore_wait(barrier, 7 + 7 + 3)

    def gather(src, buf, n):
        def g(i, a, b, to):
            return remote(a, b, gs_sem.at[n, i], gr_sem.at[n, i], head_to=to)

        mine = buf.at[pl.ds(2 * head, 2)]
        s_down, s_up = buf.at[pl.ds(2 * down, 2)], buf.at[pl.ds(2 * up, 2)]
        far0, far1 = buf.at[pl.ds(2 * far, 1)], buf.at[pl.ds(2 * far + 1, 1)]
        d0, u1 = buf.at[pl.ds(2 * down, 1)], buf.at[pl.ds(2 * up + 1, 1)]
        return [
            g(0, src, mine, sib),
            g(1, src, mine, up),
            g(2, src, mine, down),
            g(3, s_down, s_down, sib),
            g(4, d0, d0, up),
            g(5, s_up, s_up, sib),
            g(6, u1, u1, down),
            g(7, far0, far0, sib),
            g(8, far1, far1, sib),
        ]

    gk = gather(k_in, kbuf, 0)
    gq = gather(q_in, qbuf, 1)
    for i in (1, 2, 0):
        gk[i].start()

    copies[0].wait()
    copies[1].wait()

    @pl.loop(0, 16)
    def _(g):
        r = rows[:, pl.ds(pl.multiple_of(g * GROUP, GROUP), GROUP)]
        ws = [jnp.zeros(r.shape, F32) for _ in range(4)]
        for cl in range(16):
            hit = r == cl
            ws = [jnp.where(hit, table[cl, h], w) for h, w in enumerate(ws)]
        for h, w in enumerate(ws):
            sh_t[pl.ds(16 * h, 10), :] = w / jnp.sum(w, axis=0, keepdims=True)
        sh[g] = sh_t[...].T

    gk[1].wait_recv()
    gk[4].start()
    gk[3].start()
    gk[2].wait_recv()
    gk[6].start()
    gk[5].start()
    for i in (1, 2, 0):
        gq[i].start()

    for cp in v_copies:
        cp.wait()

    def states(h):
        g0 = tn(kbuf[2 * h], vbuf[2 * h])
        g1 = tn(kbuf[2 * h + 1], vbuf[2 * h + 1])
        lev1[h] = g0.astype(BF16)
        pairs[h] = (g0 + g1).reshape(8, CHUNK, 512)

    copies[2].wait()
    states(head)
    gk[0].wait_recv()
    states(sib)
    states(down)
    states(up)
    gk[4].wait_recv()
    gk[7].start()
    gk[6].wait_recv()
    gk[8].start()
    gk[3].wait_recv()
    states(down_s)
    gk[5].wait_recv()
    states(up_s)
    states(far)
    gk[7].wait_recv()
    gk[8].wait_recv()
    states(far_s)

    a2a = [
        remote(send.at[z_at(d)], recv.at[z], as_sem.at[d], ar_sem.at[d], ctx_to=ctx_z(d))
        for d in range(1, Z)
    ]

    def chunk_state(j):
        p = [pairs[h, j] for h in range(8)]
        for i in range(4):
            lev2[i, j] = p[2 * i].astype(BF16)
        p4 = [p[2 * i] + p[2 * i + 1] for i in range(4)]
        lev3[0, j] = p4[0].astype(BF16)
        lev3[1, j] = p4[2].astype(BF16)
        low = p4[0] + p4[1]
        lev4[j] = low.astype(BF16)
        return (low + p4[2] + p4[3]).astype(BF16)

    for d in (4, 3, 5, 2, 6, 1, 7):
        j = z_at(d)
        send[j] = chunk_state(j)
        a2a[d - 1].start()
    recv[z] = chunk_state(z)

    gq[1].wait_recv()
    gq[4].start()
    gq[3].start()
    gq[2].wait_recv()
    gq[6].start()
    gq[5].start()
    gq[4].wait_recv()
    gq[7].start()
    gq[6].wait_recv()
    gq[8].start()
    copies[3].wait()
    for i in (0, 3, 5, 7, 8):
        gq[i].wait_recv()

    causal = lax.broadcasted_iota(jnp.int32, (GROUP, GROUP), 0) >= lax.broadcasted_iota(
        jnp.int32, (GROUP, GROUP), 1
    )

    def weighed(part, shares, level, h):
        lane = 16 * h + level
        return part[:, h * GROUP : (h + 1) * GROUP] * shares[:, lane : lane + 1]

    @pl.loop(0, 8)
    def _(i):
        for odd in range(2):
            g = 2 * i + odd
            q, shares = qbuf[g], sh[g]
            s = jnp.where(causal, nt(q, kbuf[g]), 0.0).astype(BF16)
            near = nn(s, vbuf[g])
            if odd:
                f1 = nn(q, lev1[i])
            for h in range(4):
                t = weighed(near, shares, 0, h)
                if odd:
                    t += weighed(f1, shares, 1, h)
                total[g, :, h * GROUP : (h + 1) * GROUP] = t

    def add_far(pair, state, level):
        g = pl.ds(2 * pair, 2)
        f = nn(qbuf[g].reshape(256, 128), state)
        shares = sh[g].reshape(256, 128)
        for h in range(4):
            cols = slice(h * GROUP, (h + 1) * GROUP)
            total[g, :, cols] += weighed(f, shares, level, h).reshape(2, GROUP, GROUP)

    @pl.loop(0, 4)
    def _(m):
        add_far(2 * m + 1, lev2[m].reshape(128, 512), 2)

    @pl.loop(0, 4)
    def _(m):
        add_far(4 * (m // 2) + 2 + m % 2, lev3[m // 2].reshape(128, 512), 3)

    for cp in a2a:
        cp.wait_recv()
    r = [recv[i].astype(F32) for i in range(8)]
    s01, s23, s45, s67 = (r[2 * i] + r[2 * i + 1] for i in range(4))
    s03 = s01 + s23
    row_t[...] = (s03 + s45 + s67).astype(BF16)

    xc = [
        remote(row_t, row_r.at[x], xs_sem.at[d], xr_sem.at[d], ctx_to=(x + d) % X * Z + z)
        for d in range(1, X)
    ]
    for d in range(1, X):

        @pl.when(x + d < X)
        def _():
            xc[d - 1].start()

    pair6[0] = s01.astype(BF16)
    pair6[1] = s45.astype(BF16)
    half7[...] = s03.astype(BF16)

    def z_copy(level, d):
        to = z_at(d)
        src = (recv.at[jnp.maximum(to - 1, 0)], pair6.at[to // 4], half7)[level]
        return remote(
            src, zst.at[level, z], zs_sem.at[level, d], zr_sem.at[level, d], ctx_to=ctx_z(d)
        )

    for level in (2, 1, 0):
        for d in (4, 3, 5, 2, 6, 1, 7):

            @pl.when((z_at(d) >> level) % 2 == 1)
            def _():
                z_copy(level, d).start()

    zst[0, z] = recv[jnp.maximum(z - 1, 0)]
    zst[1, z] = pair6[z // 4]
    zst[2, z] = half7[...]

    @pl.loop(0, 4)
    def _(m):
        add_far(4 + m, lev4[...].reshape(128, 512), 4)

    for d in range(1, X):

        @pl.when(x - d >= 0)
        def _():
            xc[d - 1].wait_recv()

    def b_copy(level, d):
        src = (row_r.at[jnp.maximum(x - 1, 0)], xst.at[1, z])[level]
        return remote(
            src, xst.at[level, z], bs_sem.at[level, d], br_sem.at[level, d], ctx_to=ctx_z(d)
        )

    def level_on(level):
        return (x >> level) % 2 == 1

    @pl.when(level_on(1))
    def _():
        xst[1, z] = (row_r[0].astype(F32) + row_r[1].astype(F32)).astype(BF16)
        for d in (4, 3, 5, 2, 6, 1, 7):
            b_copy(1, d).start()

    @pl.when(level_on(0))
    def _():
        xst[0, z] = row_r[x - 1]
        for d in (4, 3, 5, 2, 6, 1, 7):
            b_copy(0, d).start()

    for level in range(2):

        @pl.when(jnp.logical_not(level_on(level)))
        def _():
            xst[level] = jnp.zeros((8, CHUNK, 512), BF16)

    @pl.loop(0, 16)
    def _(g):
        q, shares = qbuf[g].astype(F32), sh[g]
        for h in range(4):
            for level in range(2):
                lane = 16 * h + 8 + level
                qs[h, g, :, level * 128 : (level + 1) * 128] = (
                    q * shares[:, lane : lane + 1]
                ).astype(BF16)

    for level in (2, 1, 0):

        @pl.when((z >> level) % 2 == 1)
        def _():
            for d in range(1, Z):
                z_copy(level, d).wait_recv()

            @pl.loop(0, 8)
            def _(m):
                add_far(m, zst[level].reshape(128, 512), 5 + level)

    for level in range(2):

        @pl.when(level_on(level))
        def _():
            for d in range(1, Z):
                b_copy(level, d).wait_recv()

    def o_copy(i):
        g = pl.ds(4 * i, 4)
        return pltpu.make_async_copy(obuf.at[g], out.at[g], o_sem.at[i])

    @pl.loop(0, 4)
    def _(i):
        g = pl.ds(4 * i, 4)
        for h in range(4):
            cols = slice(h * GROUP, (h + 1) * GROUP)
            f = nn(qs[h, g].reshape(512, 256), xst[:, :, :, cols].reshape(256, GROUP))
            obuf[g, :, cols] = (total[g, :, cols] + f.reshape(4, GROUP, GROUP)).astype(BF16)
        o_copy(i).start()

    for cp in gk + gq + a2a:
        cp.wait_send()
    for d in range(1, X):

        @pl.when(x + d < X)
        def _():
            xc[d - 1].wait_send()

    for level in range(3):
        for d in range(1, Z):

            @pl.when((z_at(d) >> level) % 2 == 1)
            def _():
                z_copy(level, d).wait_send()

    for level in range(2):

        @pl.when(level_on(level))
        def _():
            for d in range(1, Z):
                b_copy(level, d).wait_send()

    for i in range(4):
        o_copy(i).wait()


def local(queries, keys, values, tier_weight_rows, level_table):
    tokens, columns = values.shape
    groups = tokens // GROUP
    anywhere = pl.BlockSpec(memory_space=pl.ANY)
    vm = pltpu.VMEM
    out = pl.pallas_call(
        kernel,
        out_shape=jax.ShapeDtypeStruct((groups, GROUP, columns), BF16),
        in_specs=[anywhere] * 5,
        out_specs=anywhere,
        scratch_shapes=[
            vm((16, GROUP, 128), BF16),
            vm((16, GROUP, 128), BF16),
            vm((16, GROUP, 512), BF16),
            vm((10, 2048), jnp.int32),
            pltpu.SMEM((16, 4), F32),
            vm((GROUP, GROUP), F32),
            vm((16, GROUP, GROUP), F32),
            vm((16, GROUP, 512), F32),
            vm((8, 8, CHUNK, 512), F32),
            vm((8, 128, 512), BF16),
            vm((4, 8, CHUNK, 512), BF16),
            vm((2, 8, CHUNK, 512), BF16),
            vm((8, CHUNK, 512), BF16),
            vm((8, CHUNK, 512), BF16),
            vm((8, CHUNK, 512), BF16),
            vm((2, CHUNK, 512), BF16),
            vm((CHUNK, 512), BF16),
            vm((CHUNK, 512), BF16),
            vm((4, CHUNK, 512), BF16),
            vm((3, 8, CHUNK, 512), BF16),
            vm((2, 8, CHUNK, 512), BF16),
            vm((4, 16, GROUP, 256), BF16),
            vm((16, GROUP, 512), BF16),
            DMA((4,)),
            DMA((8,)),
            DMA((4,)),
            DMA((2, 9)),
            DMA((2, 9)),
            DMA((8,)),
            DMA((8,)),
            DMA((3, 8)),
            DMA((3, 8)),
            DMA((4,)),
            DMA((4,)),
            DMA((2, 8)),
            DMA((2, 8)),
        ],
        compiler_params=pltpu.CompilerParams(collective_id=0, has_side_effects=True),
    )(
        queries.reshape(2, GROUP, 128),
        keys.reshape(2, GROUP, 128),
        values.reshape(groups, GROUP, columns),
        tier_weight_rows,
        level_table,
    )
    return out.reshape(tokens, columns)


def solution(mesh):
    return jax.shard_map(
        local,
        mesh=mesh,
        in_specs=(
            P(("ctx", "head"), None),
            P(("ctx", "head"), None),
            P("ctx", "head"),
            P(None, "ctx"),
            P(None, "head"),
        ),
        out_specs=P("ctx", "head"),
        check_vma=False,
    )
```

time: 161 us -> 49.1 us (0.30)
  local copies, waits for them, and re-layouts: 51.5 us -> 4.4 us
  Pallas kernels: 0 us -> 44.5 us
  matrix products: 37.1 us -> 0 us
  blocking collectives: 29.7 us -> 0 us
  waiting for transfers between devices: 26.8 us -> 0 us
  starting transfers between devices: 13.7 us -> 0 us
    pallas_call x0 -> x1, Pallas kernels: none -> 44.5 us  [local(): pl.pallas_call(kernel, out_shape=jax.ShapeDtypeStruct((groups, GROUP, col...]
    another operation x9 -> x0, local copies, waits for them, and re-layouts: 43.1 us -> none  [the longest x5 26.9 us: weigh(): part.reshape(tok_rows, head_count, head_width) * share[level][:, :, None]]
    dot_general x12 -> x0, matrix products: 37.1 us -> none  [the longest x5 21.4 us: local(): jnp.dot(q_whole, cumulative_memory, preferred_element_type=jnp.float32)]
    all_gather x4 -> x0, blocking collectives: 29.7 us -> none  [all_blocks(): parts = lax.all_gather(parts, axes[k])]
    ppermute x5 -> x0, waiting for transfers between devices: 26.8 us -> none  [swapped(): return lax.ppermute(value, axis, pairs)]
    ppermute x5 -> x0, starting transfers between devices: 13.7 us -> none  [swapped(): return lax.ppermute(value, axis, pairs)]
    convert_element_type x1 -> x0, local copies, waits for them, and re-layouts: 2.51 us -> none  [local(): return total.astype(jnp.bfloat16)]
    all_gather x1 -> x0, local copies, waits for them, and re-layouts: 2.04 us -> none  [all_blocks(): parts = lax.all_gather(parts, axes[k])]
  transfers between devices with their start and end apart: 5 -> 0, of which waited for: 4 -> 0; matrix products, arithmetic and copies ran while one was open for 44% -> 0% of each run, Pallas kernels for 0% -> 0%
where the time goes in v1:
time: 49.1 us; the launch traced here: 48.9 us
  Pallas kernels  44.5 us (91%)
  local copies, waits for them, and re-layouts  4.4 us (9%)
    pallas_call x1, Pallas kernels, local(): pl.pallas_call(kernel, out_shape=jax.ShapeDtypeStruct((groups, GROUP, col...  44.5 us
    unnamed x2, local copies, waits for them, and re-layouts  4.4 us

profile of v1, /device:TPU:6, one launch (start us, length us, event | category | flops | bytes accessed | tf_op | source)
XLA Modules:
  0.0 48.9 jit_solution(12121358814098937890)
XLA Ops:
  0.0 1.4 %copy.6.table_in = f32[16,4]{1,0:T(8,128)} copy(f32[16,4]{0,1:T(4,128)} %param.9) | data formatting | bytes 512 | tf_op args[4]
  1.4 44.5 %shard_map.55 = bf16[16,128,512]{2,1,0:T(8,128)(2,1)} custom-call(bf16[2,128,128]{2,1,0:T(8,128)(2,1)} %bitcast.6, bf16[2,128,128]{2,1,0:T(8,128)(2,1)} %bitcast.7, bf16[16,128,512]{2,1,0:T(8,128)(2,1)} %bitcast.5, s32[10,2048]{1,0:T(8,128)} %rows_in.1, f32[16,4]{1,0:T(8,128)} %copy.6.table_in), custom_call_target="tpu_custom_call" | custom-call | tf_op jit(solution)/shard_map/pallas_call | solution.py:386
  45.9 3.0 %copy.8 = bf16[2048,512]{1,0:T(8,128)(2,1)} copy(bf16[2048,512]{1,0:T(8,128)(2,1)} %bitcast.4) | data formatting | bytes 4194304

commit v2 on v1

v2 whole, which is shorter than its diff:
```python
import functools

import jax
import jax.numpy as jnp
from jax import lax
from jax.experimental import pallas as pl
from jax.experimental.pallas import tpu as pltpu
from jax.sharding import PartitionSpec as P

GROUP = 128
X, Y, Z = 4, 4, 8
CHUNK = 64
F32, BF16 = jnp.float32, jnp.bfloat16
DMA = pltpu.SemaphoreType.DMA


def nt(a, b):
    return lax.dot_general(a, b, (((1,), (1,)), ((), ())), preferred_element_type=F32)


def nn(a, b):
    return jnp.dot(a, b, preferred_element_type=F32)


def kernel(
    q_in, k_in, v_in, rows_in, table_in, out,
    qbuf, kbuf, vbuf, vt, rows, table, sh, total, pairs, lev1, lev2, lev3, lev4,
    send, recv, pair6, half7, row_f, row_b, row_r, zst, xst, obuf,
    loc_sem, v_sem, o_sem, gs_sem, gr_sem, as_sem, ar_sem, zs_sem, zr_sem,
    xs_sem, xr_sem, bs_sem, br_sem,
):
    ctx = lax.axis_index("ctx")
    head = lax.axis_index("head")
    x, z = ctx // Z, ctx % Z
    y, c = head // 2, head % 2
    sib = y * 2 + 1 - c
    up = ((y + 1) % Y) * 2 + c
    down = ((y + 3) % Y) * 2 + c
    far = ((y + 2) % Y) * 2 + c
    up_s, down_s, far_s = (((y + d) % Y) * 2 + 1 - c for d in (1, 3, 2))

    def remote(src, dst, ss, rs, ctx_to=ctx, head_to=head):
        return pltpu.make_async_remote_copy(
            src, dst, ss, rs, device_id=(ctx_to, head_to), device_id_type=pl.DeviceIdType.MESH
        )

    def z_at(d):
        return (z + d) % Z

    def ctx_z(d):
        return x * Z + z_at(d)

    copies = [
        pltpu.make_async_copy(rows_in, rows, loc_sem.at[0]),
        pltpu.make_async_copy(table_in, table, loc_sem.at[1]),
        pltpu.make_async_copy(k_in, kbuf.at[pl.ds(2 * head, 2)], loc_sem.at[2]),
        pltpu.make_async_copy(q_in, qbuf.at[pl.ds(2 * head, 2)], loc_sem.at[3]),
    ]
    v_copies = [
        pltpu.make_async_copy(v_in.at[pl.ds(2 * i, 2)], vbuf.at[pl.ds(2 * i, 2)], v_sem.at[i])
        for i in range(8)
    ]

    barrier = pltpu.get_barrier_semaphore()
    partners = [(ctx, to) for to in (sib, up, down)]
    partners += [(ctx_z(d), head) for d in range(1, Z)]
    partners += [((x + d) % X * Z + z, head) for d in range(1, X)]
    for to in partners:
        pl.semaphore_signal(barrier, 1, device_id=to, device_id_type=pl.DeviceIdType.MESH)
    for cp in copies + v_copies:
        cp.start()
    pl.semaphore_wait(barrier, len(partners))

    def gather(src, buf, n):
        def g(i, a, b, to):
            return remote(a, b, gs_sem.at[n, i], gr_sem.at[n, i], head_to=to)

        mine = buf.at[pl.ds(2 * head, 2)]
        s_down, s_up = buf.at[pl.ds(2 * down, 2)], buf.at[pl.ds(2 * up, 2)]
        far0, far1 = buf.at[pl.ds(2 * far, 1)], buf.at[pl.ds(2 * far + 1, 1)]
        d0, u1 = buf.at[pl.ds(2 * down, 1)], buf.at[pl.ds(2 * up + 1, 1)]
        return [
            g(0, src, mine, sib),
            g(1, src, mine, up),
            g(2, src, mine, down),
            g(3, s_down, s_down, sib),
            g(4, d0, d0, up),
            g(5, s_up, s_up, sib),
            g(6, u1, u1, down),
            g(7, far0, far0, sib),
            g(8, far1, far1, sib),
        ]

    gk = gather(k_in, kbuf, 0)
    gq = gather(q_in, qbuf, 1)
    for i in (1, 2, 0):
        gk[i].start()

    for cp in v_copies:
        cp.wait()

    @pl.loop(0, 8)
    def _(i):
        for odd in range(2):
            vt[i, :, odd * 128 : (odd + 1) * 128] = vbuf[2 * i + odd].T

    gk[1].wait_recv()
    gk[4].start()
    gk[3].start()
    gk[2].wait_recv()
    gk[6].start()
    gk[5].start()
    for i in (1, 2, 0):
        gq[i].start()

    copies[0].wait()
    copies[1].wait()

    @pl.loop(0, 8)
    def _(i):
        r = rows[:, pl.ds(pl.multiple_of(i * 256, 256), 256)]
        ws = [jnp.zeros(r.shape, F32) for _ in range(4)]
        for cl in range(16):
            hit = r == cl
            ws = [jnp.where(hit, table[h, cl], w) for h, w in enumerate(ws)]
        for h, w in enumerate(ws):
            sh[i, pl.ds(16 * h, 10), :] = w / jnp.sum(w, axis=0, keepdims=True)


    def states(h):
        g0 = nn(vt[h, :, :128], kbuf[2 * h])
        g1 = nn(vt[h, :, 128:], kbuf[2 * h + 1])
        lev1[h] = g0.astype(BF16)
        pairs[h] = (g0 + g1).reshape(8, CHUNK, 128)

    copies[2].wait()
    states(head)
    gk[0].wait_recv()
    states(sib)
    states(down)
    states(up)
    gk[4].wait_recv()
    gk[7].start()
    gk[6].wait_recv()
    gk[8].start()
    gk[3].wait_recv()
    states(down_s)
    gk[5].wait_recv()
    states(up_s)
    states(far)
    gk[7].wait_recv()
    gk[8].wait_recv()
    states(far_s)

    a2a = [
        remote(send.at[z_at(d)], recv.at[z], as_sem.at[d], ar_sem.at[d], ctx_to=ctx_z(d))
        for d in range(1, Z)
    ]

    def chunk_state(j):
        p = [pairs[h, j] for h in range(8)]
        for i in range(4):
            lev2[i, j] = p[2 * i].astype(BF16)
        p4 = [p[2 * i] + p[2 * i + 1] for i in range(4)]
        lev3[0, j] = p4[0].astype(BF16)
        lev3[1, j] = p4[2].astype(BF16)
        low = p4[0] + p4[1]
        lev4[j] = low.astype(BF16)
        send[j] = (low + p4[2] + p4[3]).astype(BF16)

    for d in (4, 3, 5, 2, 6, 1, 7):
        chunk_state(z_at(d))
        a2a[d - 1].start()
    chunk_state(z)
    recv[z] = send[z]

    next_z = remote(send, zst.at[0], zs_sem.at[0, 0], zr_sem.at[0, 0], ctx_to=ctx_z(1))

    @pl.when(z % 2 == 0)
    def _():
        next_z.start()

    causal = lax.broadcasted_iota(jnp.int32, (GROUP, GROUP), 0) >= lax.broadcasted_iota(
        jnp.int32, (GROUP, GROUP), 1
    )
    heads = [slice(h * GROUP, (h + 1) * GROUP) for h in range(4)]

    def share(i, level, h):
        return sh[i, 16 * h + level : 16 * h + level + 1, :]

    def add_far(i, state, level):
        f = nt(state, qbuf[pl.ds(2 * i, 2)].reshape(256, 128))
        for h in range(4):
            total[i, heads[h], :] += f[heads[h]] * share(i, level, h)

    def near(i):
        for odd in range(2):
            g = 2 * i + odd
            cols = slice(odd * GROUP, (odd + 1) * GROUP)
            q = qbuf[g]
            s = jnp.where(causal, nt(q, kbuf[g]), 0.0).astype(BF16)
            f0 = nt(vt[i, :, cols], s)
            if odd:
                f1 = nt(lev1[i], q)
            for h in range(4):
                t = f0[heads[h]] * share(i, 0, h)[:, cols]
                if odd:
                    t += f1[heads[h]] * share(i, 1, h)[:, cols]
                total[i, heads[h], cols] = t

        @pl.when(i % 2 == 1)
        def _():
            add_far(i, lev2[i // 2].reshape(512, 128), 2)

        @pl.when(i // 2 % 2 == 1)
        def _():
            add_far(i, lev3[i // 4].reshape(512, 128), 3)

        @pl.when(i // 4 == 1)
        def _():
            add_far(i, lev4[...].reshape(512, 128), 4)

    copies[3].wait()
    near(head)
    gq[1].wait_recv()
    gq[4].start()
    gq[3].start()
    gq[2].wait_recv()
    gq[6].start()
    gq[5].start()
    gq[0].wait_recv()
    near(sib)

    @pl.loop(0, 2)
    def _(e):
        near((y + 3 + 2 * e) % Y * 2 + c)

    gq[4].wait_recv()
    gq[7].start()
    gq[6].wait_recv()
    gq[8].start()

    for cp in a2a:
        cp.wait_recv()
    r = [recv[i].astype(F32) for i in range(8)]
    s01, s23, s45, s67 = (r[2 * i] + r[2 * i + 1] for i in range(4))
    s03 = s01 + s23
    row = s03 + s45 + s67
    row_f[...] = row

    def x_copy(to):
        return remote(row_f, row_r.at[x], xs_sem.at[to], xr_sem.at[x], ctx_to=to * Z + z)

    @pl.when(x < 2)
    def _():
        for to in (2, 3):
            x_copy(to).start()

    row_b[...] = row.astype(BF16)
    pair6[0] = s01.astype(BF16)
    pair6[1] = s45.astype(BF16)
    half7[...] = s03.astype(BF16)

    def t_copy(d):
        to = (x + 1) % X * Z + z_at(d)
        return remote(row_b, xst.at[0, z], bs_sem.at[0, d], br_sem.at[0, d], ctx_to=to)

    def z_copy(level, d):
        src = (None, pair6.at[z_at(d) // 4], half7)[level]
        return remote(
            src, zst.at[level, z], zs_sem.at[level, d], zr_sem.at[level, d], ctx_to=ctx_z(d)
        )

    order = (4, 3, 5, 2, 6, 1, 7)
    for level in (2, 1):
        for d in order:

            @pl.when((z_at(d) >> level) % 2 == 1)
            def _():
                z_copy(level, d).start()

    @pl.when(x % 2 == 0)
    def _():
        for d in order + (0,):
            t_copy(d).start()

    zst[1, z] = pair6[z // 4]
    zst[2, z] = half7[...]

    gq[3].wait_recv()
    gq[5].wait_recv()

    @pl.loop(0, 2)
    def _(e):
        near((y + 3 + 2 * e) % Y * 2 + 1 - c)

    def b_copy(d):
        return remote(
            xst.at[1, z], xst.at[1, z], bs_sem.at[1, d], br_sem.at[1, d], ctx_to=ctx_z(d)
        )

    @pl.when(x >= 2)
    def _():
        for s in range(2):
            remote(row_f, row_r.at[s], xs_sem.at[s], xr_sem.at[s]).wait_recv()
        xst[1, z] = (row_r[0] + row_r[1]).astype(BF16)
        for d in order:
            b_copy(d).start()

    @pl.when(x < 2)
    def _():
        xst[1] = jnp.zeros((8, CHUNK, 128), BF16)

    @pl.when(x % 2 == 0)
    def _():
        xst[0] = jnp.zeros((8, CHUNK, 128), BF16)

    gq[7].wait_recv()
    gq[8].wait_recv()

    @pl.loop(0, 2)
    def _(e):
        near((y + 2) % Y * 2 + e)

    @pl.when(z % 2 == 1)
    def _():
        next_z.wait_recv()

        @pl.loop(0, 8)
        def _(m):
            add_far(m, zst[0].reshape(512, 128), 5)

    for level in (2, 1):

        @pl.when((z >> level) % 2 == 1)
        def _():
            for d in range(1, Z):
                z_copy(level, d).wait_recv()

            @pl.loop(0, 8)
            def _(m):
                add_far(m, zst[level].reshape(512, 128), 5 + level)

    @pl.when(x % 2 == 1)
    def _():
        for d in range(Z):
            t_copy(d).wait_recv()

    @pl.when(x >= 2)
    def _():
        for d in range(1, Z):
            b_copy(d).wait_recv()

    def o_copy(i):
        g = pl.ds(2 * i, 2)
        return pltpu.make_async_copy(obuf.at[g], out.at[g], o_sem.at[i])

    @pl.loop(0, 8)
    def _(i):
        q = qbuf[pl.ds(2 * i, 2)].reshape(256, 128)
        f8 = nt(xst[0].reshape(512, 128), q)
        f9 = nt(xst[1].reshape(512, 128), q)
        for h in range(4):
            t = total[i, heads[h], :] + f8[heads[h]] * share(i, 8, h) + f9[heads[h]] * share(i, 9, h)
            obuf[pl.ds(2 * i, 2), :, heads[h]] = t.astype(BF16).T.reshape(2, GROUP, GROUP)
        o_copy(i).start()

    for cp in gk + gq + a2a:
        cp.wait_send()

    @pl.when(z % 2 == 0)
    def _():
        next_z.wait_send()

    @pl.when(x < 2)
    def _():
        for to in (2, 3):
            x_copy(to).wait_send()

    for level in (2, 1):
        for d in range(1, Z):

            @pl.when((z_at(d) >> level) % 2 == 1)
            def _():
                z_copy(level, d).wait_send()

    @pl.when(x % 2 == 0)
    def _():
        for d in range(Z):
            t_copy(d).wait_send()

    @pl.when(x >= 2)
    def _():
        for d in range(1, Z):
            b_copy(d).wait_send()

    for i in range(8):
        o_copy(i).wait()


def local(queries, keys, values, tier_weight_rows, level_table):
    tokens, columns = values.shape
    groups = tokens // GROUP
    anywhere = pl.BlockSpec(memory_space=pl.ANY)
    vm = pltpu.VMEM
    out = pl.pallas_call(
        kernel,
        out_shape=jax.ShapeDtypeStruct((groups, GROUP, columns), BF16),
        in_specs=[anywhere] * 5,
        out_specs=anywhere,
        scratch_shapes=[
            vm((16, GROUP, 128), BF16),
            vm((16, GROUP, 128), BF16),
            vm((16, GROUP, 512), BF16),
            vm((8, 512, 256), BF16),
            vm((10, 2048), jnp.int32),
            pltpu.SMEM((4, 16), F32),
            vm((8, 64, 256), F32),
            vm((8, 512, 256), F32),
            vm((8, 8, CHUNK, 128), F32),
            vm((8, 512, 128), BF16),
            vm((4, 8, CHUNK, 128), BF16),
            vm((2, 8, CHUNK, 128), BF16),
            vm((8, CHUNK, 128), BF16),
            vm((8, CHUNK, 128), BF16),
            vm((8, CHUNK, 128), BF16),
            vm((2, CHUNK, 128), BF16),
            vm((CHUNK, 128), BF16),
            vm((CHUNK, 128), F32),
            vm((CHUNK, 128), BF16),
            vm((2, CHUNK, 128), F32),
            vm((3, 8, CHUNK, 128), BF16),
            vm((2, 8, CHUNK, 128), BF16),
            vm((16, GROUP, 512), BF16),
            DMA((4,)),
            DMA((8,)),
            DMA((8,)),
            DMA((2, 9)),
            DMA((2, 9)),
            DMA((8,)),
            DMA((8,)),
            DMA((3, 8)),
            DMA((3, 8)),
            DMA((4,)),
            DMA((2,)),
            DMA((2, 8)),
            DMA((2, 8)),
        ],
        compiler_params=pltpu.CompilerParams(collective_id=0, has_side_effects=True),
    )(
        queries.reshape(2, GROUP, 128),
        keys.reshape(2, GROUP, 128),
        values.reshape(groups, GROUP, columns),
        tier_weight_rows,
        level_table.T,
    )
    return out.reshape(tokens, columns)


def solution(mesh):
    return jax.shard_map(
        local,
        mesh=mesh,
        in_specs=(
            P(("ctx", "head"), None),
            P(("ctx", "head"), None),
            P("ctx", "head"),
            P(None, "ctx"),
            P(None, "head"),
        ),
        out_specs=P("ctx", "head"),
        check_vma=False,
    )
```

time: 49.1 us -> 42.4 us (0.86)
  the two profiles are of different devices: /device:TPU:6 before, /device:TPU:4 now
where the time goes in v2:
time: 42.4 us; the launch traced here: 42.3 us
  Pallas kernels  39.2 us (92%)
  local copies, waits for them, and re-layouts  3.05 us (7%)
    pallas_call x1, Pallas kernels, local(): pl.pallas_call(kernel, out_shape=jax.ShapeDtypeStruct((groups, GROUP, col...  39.2 us
    unnamed x1, local copies, waits for them, and re-layouts  3.05 us

profile of v2, /device:TPU:4, one launch (start us, length us, event | category | flops | bytes accessed | tf_op | source)
XLA Modules:
  0.0 42.3 jit_solution(14947821313795278747)
XLA Ops:
  0.0 39.2 %shard_map.55 = bf16[16,128,512]{2,1,0:T(8,128)(2,1)} custom-call(bf16[2,128,128]{2,1,0:T(8,128)(2,1)} %bitcast.7, bf16[2,128,128]{2,1,0:T(8,128)(2,1)} %bitcast.8, bf16[16,128,512]{2,1,0:T(8,128)(2,1)} %bitcast.6, s32[10,2048]{1,0:T(8,128)} %rows_in.1, f32[4,16]{1,0:T(4,128)} %bitcast.9), custom_call_target="tpu_custom_call" | custom-call | tf_op jit(solution)/shard_map/pallas_call | solution.py:406
  39.2 3.0 %copy.7 = bf16[2048,512]{1,0:T(8,128)(2,1)} copy(bf16[2048,512]{1,0:T(8,128)(2,1)} %bitcast.5) | data formatting | bytes 4194304

commit v3 on v2

--- a/solution.py
+++ b/solution.py
@@ -23,11 +23,12 @@
 
 
 def kernel(
-    q_in, k_in, v_in, rows_in, table_in, out,
-    qbuf, kbuf, vbuf, vt, rows, table, sh, total, pairs, lev1, lev2, lev3, lev4,
-    send, recv, pair6, half7, row_f, row_b, row_r, zst, xst, obuf,
-    loc_sem, v_sem, o_sem, gs_sem, gr_sem, as_sem, ar_sem, zs_sem, zr_sem,
-    xs_sem, xr_sem, bs_sem, br_sem,
+    q_in, k_in, v_in, rows_in, table_in,
+    qbuf, sh, total, xst,
+    kbuf, vbuf, vt, rows, table, pairs, lev1, lev2, lev3, lev4,
+    send, recv, pair6, half7, row_f, row_b, row_r, both, zst,
+    loc_sem, v_sem, gs_sem, gr_sem, as_sem, ar_sem, zs_sem, zr_sem,
+    xs_sem, xr_sem, bs_sem, br_sem, in_sem,
 ):
     ctx = lax.axis_index("ctx")
     head = lax.axis_index("head")
@@ -61,12 +62,13 @@
         for i in range(8)
     ]
 
+    mesh_id = pl.DeviceIdType.MESH
     barrier = pltpu.get_barrier_semaphore()
-    partners = [(ctx, to) for to in (sib, up, down)]
-    partners += [(ctx_z(d), head) for d in range(1, Z)]
-    partners += [((x + d) % X * Z + z, head) for d in range(1, X)]
+    next_x = [((x + d) % X * Z + z, head) for d in (1, X - 1)]
+    next_z = [(ctx_z(d), head) for d in (1, Z - 1)]
+    partners = [(ctx, to) for to in (sib, up, down)] + next_z + next_x
     for to in partners:
-        pl.semaphore_signal(barrier, 1, device_id=to, device_id_type=pl.DeviceIdType.MESH)
+        pl.semaphore_signal(barrier, 1, device_id=to, device_id_type=mesh_id)
     for cp in copies + v_copies:
         cp.start()
     pl.semaphore_wait(barrier, len(partners))
@@ -75,26 +77,38 @@
         def g(i, a, b, to):
             return remote(a, b, gs_sem.at[n, i], gr_sem.at[n, i], head_to=to)
 
-        mine = buf.at[pl.ds(2 * head, 2)]
-        s_down, s_up = buf.at[pl.ds(2 * down, 2)], buf.at[pl.ds(2 * up, 2)]
-        far0, far1 = buf.at[pl.ds(2 * far, 1)], buf.at[pl.ds(2 * far + 1, 1)]
-        d0, u1 = buf.at[pl.ds(2 * down, 1)], buf.at[pl.ds(2 * up + 1, 1)]
+        def part(h, half):
+            return buf.at[pl.ds(2 * h + half, 1)]
+
+        def whole(h):
+            return buf.at[pl.ds(2 * h, 2)]
+
+        first, second = src.at[pl.ds(0, 1)], src.at[pl.ds(1, 1)]
         return [
-            g(0, src, mine, sib),
-            g(1, src, mine, up),
-            g(2, src, mine, down),
-            g(3, s_down, s_down, sib),
-            g(4, d0, d0, up),
-            g(5, s_up, s_up, sib),
-            g(6, u1, u1, down),
-            g(7, far0, far0, sib),
-            g(8, far1, far1, sib),
+            g(0, src, whole(head), sib),
+            g(1, first, part(head, 0), up),
+            g(2, second, part(head, 1), up),
+            g(3, second, part(head, 1), down),
+            g(4, first, part(head, 0), down),
+            g(5, part(down, 0), part(down, 0), up),
+            g(6, part(up, 1), part(up, 1), down),
+            g(7, whole(down), whole(down), sib),
+            g(8, whole(up), whole(up), sib),
+            g(9, part(far, 0), part(far, 0), sib),
+            g(10, part(far, 1), part(far, 1), sib),
         ]
+
+    def step(copies, *pairs):
+        for landed, started in pairs:
+            copies[landed].wait_recv()
+            copies[started].start()
 
     gk = gather(k_in, kbuf, 0)
     gq = gather(q_in, qbuf, 1)
-    for i in (1, 2, 0):
+    for i in (1, 3, 2, 4, 0):
         gk[i].start()
+    for to in next_z + next_x:
+        pl.semaphore_signal(in_sem.at[0], 1, device_id=to, device_id_type=mesh_id)
 
     for cp in v_copies:
         cp.wait()
@@ -103,15 +117,6 @@
     def _(i):
         for odd in range(2):
             vt[i, :, odd * 128 : (odd + 1) * 128] = vbuf[2 * i + odd].T
-
-    gk[1].wait_recv()
-    gk[4].start()
-    gk[3].start()
-    gk[2].wait_recv()
-    gk[6].start()
-    gk[5].start()
-    for i in (1, 2, 0):
-        gq[i].start()
 
     copies[0].wait()
     copies[1].wait()
@@ -126,6 +131,16 @@
         for h, w in enumerate(ws):
             sh[i, pl.ds(16 * h, 10), :] = w / jnp.sum(w, axis=0, keepdims=True)
 
+    pl.semaphore_wait(in_sem.at[0], 4)
+    for d in (2, Z - 2):
+        pl.semaphore_signal(
+            in_sem.at[1], 1, device_id=(ctx_z(d), head), device_id_type=mesh_id
+        )
+
+    step(gk, (1, 5), (3, 6), (2, 7), (4, 8))
+    for i in (1, 3, 2, 4):
+        gq[i].start()
+
 
     def states(h):
         g0 = nn(vt[h, :, :128], kbuf[2 * h])
@@ -135,22 +150,21 @@
 
     copies[2].wait()
     states(head)
+    states(down)
+    states(up)
+    step(gk, (5, 9), (6, 10))
+    gq[0].start()
+    states(far)
     gk[0].wait_recv()
     states(sib)
-    states(down)
-    states(up)
-    gk[4].wait_recv()
-    gk[7].start()
-    gk[6].wait_recv()
-    gk[8].start()
-    gk[3].wait_recv()
+    gk[7].wait_recv()
     states(down_s)
-    gk[5].wait_recv()
+    gk[8].wait_recv()
     states(up_s)
-    states(far)
-    gk[7].wait_recv()
-    gk[8].wait_recv()
+    gk[9].wait_recv()
+    gk[10].wait_recv()
     states(far_s)
+    pl.semaphore_wait(in_sem.at[1], 2)
 
     a2a = [
         remote(send.at[z_at(d)], recv.at[z], as_sem.at[d], ar_sem.at[d], ctx_to=ctx_z(d))
@@ -174,11 +188,11 @@
     chunk_state(z)
     recv[z] = send[z]
 
-    next_z = remote(send, zst.at[0], zs_sem.at[0, 0], zr_sem.at[0, 0], ctx_to=ctx_z(1))
+    z_next = remote(send, zst.at[0], zs_sem.at[0, 0], zr_sem.at[0, 0], ctx_to=ctx_z(1))
 
     @pl.when(z % 2 == 0)
     def _():
-        next_z.start()
+        z_next.start()
 
     causal = lax.broadcasted_iota(jnp.int32, (GROUP, GROUP), 0) >= lax.broadcasted_iota(
         jnp.int32, (GROUP, GROUP), 1
@@ -222,12 +236,7 @@
 
     copies[3].wait()
     near(head)
-    gq[1].wait_recv()
-    gq[4].start()
-    gq[3].start()
-    gq[2].wait_recv()
-    gq[6].start()
-    gq[5].start()
+    step(gq, (1, 5), (3, 6), (2, 7), (4, 8))
     gq[0].wait_recv()
     near(sib)
 
@@ -235,10 +244,7 @@
     def _(e):
         near((y + 3 + 2 * e) % Y * 2 + c)
 
-    gq[4].wait_recv()
-    gq[7].start()
-    gq[6].wait_recv()
-    gq[8].start()
+    step(gq, (5, 9), (6, 10))
 
     for cp in a2a:
         cp.wait_recv()
@@ -251,9 +257,10 @@
     def x_copy(to):
         return remote(row_f, row_r.at[x], xs_sem.at[to], xr_sem.at[x], ctx_to=to * Z + z)
 
-    @pl.when(x < 2)
-    def _():
-        for to in (2, 3):
+    for to, sender in ((3, x < 2), (1, x == 0)):
+
+        @pl.when(sender)
+        def _():
             x_copy(to).start()
 
     row_b[...] = row.astype(BF16)
@@ -287,23 +294,34 @@
     zst[1, z] = pair6[z // 4]
     zst[2, z] = half7[...]
 
-    gq[3].wait_recv()
-    gq[5].wait_recv()
+    gq[7].wait_recv()
+    gq[8].wait_recv()
 
     @pl.loop(0, 2)
     def _(e):
         near((y + 3 + 2 * e) % Y * 2 + 1 - c)
 
     def b_copy(d):
-        return remote(
-            xst.at[1, z], xst.at[1, z], bs_sem.at[1, d], br_sem.at[1, d], ctx_to=ctx_z(d)
-        )
-
-    @pl.when(x >= 2)
-    def _():
-        for s in range(2):
-            remote(row_f, row_r.at[s], xs_sem.at[s], xr_sem.at[s]).wait_recv()
-        xst[1, z] = (row_r[0] + row_r[1]).astype(BF16)
+        to = jnp.where(x == 1, ctx_z(d) + Z, ctx_z(d))
+        return remote(both, xst.at[1, z], bs_sem.at[1, d], br_sem.at[1, d], ctx_to=to)
+
+    def x_wait(s):
+        remote(row_f, row_r.at[s], xs_sem.at[s], xr_sem.at[s]).wait_recv()
+
+    @pl.when(x == 1)
+    def _():
+        x_wait(0)
+        both[...] = (row_r[0] + row_f[...]).astype(BF16)
+        for d in order + (0,):
+            b_copy(d).start()
+
+    @pl.when(x == 3)
+    def _():
+        x_wait(0)
+        x_wait(1)
+        t = (row_r[0] + row_r[1]).astype(BF16)
+        both[...] = t
+        xst[1, z] = t
         for d in order:
             b_copy(d).start()
 
@@ -311,70 +329,57 @@
     def _():
         xst[1] = jnp.zeros((8, CHUNK, 128), BF16)
 
-    @pl.when(x % 2 == 0)
-    def _():
-        xst[0] = jnp.zeros((8, CHUNK, 128), BF16)
-
-    gq[7].wait_recv()
-    gq[8].wait_recv()
+    gq[9].wait_recv()
+    gq[10].wait_recv()
 
     @pl.loop(0, 2)
     def _(e):
         near((y + 2) % Y * 2 + e)
 
+    def add_all(state, level):
+        @pl.loop(0, 4)
+        def _(m):
+            for i in range(2):
+                add_far(2 * m + i, state.reshape(512, 128), level)
+
     @pl.when(z % 2 == 1)
     def _():
-        next_z.wait_recv()
-
-        @pl.loop(0, 8)
-        def _(m):
-            add_far(m, zst[0].reshape(512, 128), 5)
+        z_next.wait_recv()
+        add_all(zst[0], 5)
 
     for level in (2, 1):
-
         @pl.when((z >> level) % 2 == 1)
         def _():
             for d in range(1, Z):
                 z_copy(level, d).wait_recv()
-
-            @pl.loop(0, 8)
-            def _(m):
-                add_far(m, zst[level].reshape(512, 128), 5 + level)
+            add_all(zst[level], 5 + level)
 
     @pl.when(x % 2 == 1)
     def _():
         for d in range(Z):
             t_copy(d).wait_recv()
+        add_all(xst[0], 8)
 
     @pl.when(x >= 2)
     def _():
         for d in range(1, Z):
             b_copy(d).wait_recv()
 
-    def o_copy(i):
-        g = pl.ds(2 * i, 2)
-        return pltpu.make_async_copy(obuf.at[g], out.at[g], o_sem.at[i])
-
-    @pl.loop(0, 8)
-    def _(i):
-        q = qbuf[pl.ds(2 * i, 2)].reshape(256, 128)
-        f8 = nt(xst[0].reshape(512, 128), q)
-        f9 = nt(xst[1].reshape(512, 128), q)
-        for h in range(4):
-            t = total[i, heads[h], :] + f8[heads[h]] * share(i, 8, h) + f9[heads[h]] * share(i, 9, h)
-            obuf[pl.ds(2 * i, 2), :, heads[h]] = t.astype(BF16).T.reshape(2, GROUP, GROUP)
-        o_copy(i).start()
+    @pl.when(x == 2)
+    def _():
+        b_copy(0).wait_recv()
 
     for cp in gk + gq + a2a:
         cp.wait_send()
 
     @pl.when(z % 2 == 0)
     def _():
-        next_z.wait_send()
-
-    @pl.when(x < 2)
-    def _():
-        for to in (2, 3):
+        z_next.wait_send()
+
+    for to, sender in ((3, x < 2), (1, x == 0)):
+
+        @pl.when(sender)
+        def _():
             x_copy(to).wait_send()
 
     for level in (2, 1):
@@ -389,13 +394,34 @@
         for d in range(Z):
             t_copy(d).wait_send()
 
-    @pl.when(x >= 2)
+    @pl.when(x % 2 == 1)
     def _():
         for d in range(1, Z):
             b_copy(d).wait_send()
 
-    for i in range(8):
-        o_copy(i).wait()
+    @pl.when(x == 1)
+    def _():
+        b_copy(0).wait_send()
+
+
+def finish(qbuf, sh, total, xst, out, obuf, o_sem):
+    def o_copy(m):
+        g = pl.ds(4 * m, 4)
+        return pltpu.make_async_copy(obuf.at[g], out.at[g], o_sem.at[m])
+
+    @pl.loop(0, 4)
+    def _(m):
+        for i in (2 * m, 2 * m + 1):
+            f = nt(xst[1].reshape(512, 128), qbuf[pl.ds(2 * i, 2)].reshape(256, 128))
+            for h in range(4):
+                rows = slice(h * GROUP, (h + 1) * GROUP)
+                lane = 16 * h + 9
+                t = total[i, rows, :] + f[rows] * sh[i, lane : lane + 1, :]
+                obuf[pl.ds(2 * i, 2), :, rows] = t.astype(BF16).T.reshape(2, GROUP, GROUP)
+        o_copy(m).start()
+
+    for m in range(4):
+        o_copy(m).wait()
 
 
 def local(queries, keys, values, tier_weight_rows, level_table):
@@ -403,20 +429,24 @@
     groups = tokens // GROUP
     anywhere = pl.BlockSpec(memory_space=pl.ANY)
     vm = pltpu.VMEM
-    out = pl.pallas_call(
+    kept = (
+        vm((16, GROUP, 128), BF16),
+        vm((8, 64, 256), F32),
+        vm((8, 512, 256), F32),
+        vm((2, 8, CHUNK, 128), BF16),
+    )
+    in_vmem = [pl.BlockSpec(memory_space=pltpu.VMEM)] * len(kept)
+    parts = pl.pallas_call(
         kernel,
-        out_shape=jax.ShapeDtypeStruct((groups, GROUP, columns), BF16),
-        in_specs=[anywhere] * 5,
-        out_specs=anywhere,
+        out_shape=kept,
+        in_specs=[pl.BlockSpec(memory_space=pltpu.MemorySpace.HBM)] * 5,
+        out_specs=in_vmem,
         scratch_shapes=[
-            vm((16, GROUP, 128), BF16),
             vm((16, GROUP, 128), BF16),
             vm((16, GROUP, 512), BF16),
             vm((8, 512, 256), BF16),
             vm((10, 2048), jnp.int32),
             pltpu.SMEM((4, 16), F32),
-            vm((8, 64, 256), F32),
-            vm((8, 512, 256), F32),
             vm((8, 8, CHUNK, 128), F32),
             vm((8, 512, 128), BF16),
             vm((4, 8, CHUNK, 128), BF16),
@@ -429,14 +459,12 @@
             vm((CHUNK, 128), F32),
             vm((CHUNK, 128), BF16),
             vm((2, CHUNK, 128), F32),
+            vm((CHUNK, 128), BF16),
             vm((3, 8, CHUNK, 128), BF16),
-            vm((2, 8, CHUNK, 128), BF16),
-            vm((16, GROUP, 512), BF16),
             DMA((4,)),
             DMA((8,)),
-            DMA((8,)),
-            DMA((2, 9)),
-            DMA((2, 9)),
+            DMA((2, 11)),
+            DMA((2, 11)),
             DMA((8,)),
             DMA((8,)),
             DMA((3, 8)),
@@ -445,15 +473,29 @@
             DMA((2,)),
             DMA((2, 8)),
             DMA((2, 8)),
+            pltpu.SemaphoreType.REGULAR((2,)),
         ],
-        compiler_params=pltpu.CompilerParams(collective_id=0, has_side_effects=True),
-    )(
-        queries.reshape(2, GROUP, 128),
-        keys.reshape(2, GROUP, 128),
-        values.reshape(groups, GROUP, columns),
-        tier_weight_rows,
-        level_table.T,
-    )
+        compiler_params=pltpu.CompilerParams(
+            collective_id=0, has_side_effects=True, vmem_limit_bytes=24 * 2**20
+        ),
+    )(*(
+        pltpu.with_memory_space_constraint(arg, pltpu.MemorySpace.HBM)
+        for arg in (
+            queries.reshape(2, GROUP, 128),
+            keys.reshape(2, GROUP, 128),
+            values.reshape(groups, GROUP, columns),
+            tier_weight_rows,
+            level_table.T,
+        )
+    ))
+    out = pl.pallas_call(
+        finish,
+        out_shape=jax.ShapeDtypeStruct((groups, GROUP, columns), BF16),
+        in_specs=in_vmem,
+        out_specs=anywhere,
+        scratch_shapes=[vm((groups, GROUP, columns), BF16), DMA((4,))],
+        compiler_params=pltpu.CompilerParams(vmem_limit_bytes=12 * 2**20),
+    )(*parts)
     return out.reshape(tokens, columns)
 
 

time: 42.4 us -> 36.3 us (0.86)
  the two profiles are of different devices: /device:TPU:4 before, /device:TPU:2 now
where the time goes in v3:
time: 36.3 us; the launch traced here: 36.2 us
  Pallas kernels  36.2 us (100%)
    pallas_call x1, Pallas kernels, local(): pl.pallas_call(kernel, out_shape=kept, in_specs=[pl.BlockSpec(memory_spac...  33.9 us
    pallas_call x1, Pallas kernels, local(): pl.pallas_call(finish, out_shape=jax.ShapeDtypeStruct((groups, GROUP, col...  2.34 us

profile of v3, /device:TPU:2, one launch (start us, length us, event | category | flops | bytes accessed | tf_op | source)
XLA Modules:
  0.0 36.2 jit_solution(6553284814330276167)
XLA Ops:
  0.0 33.9 %shard_map.55 = (bf16[16,128,128]{2,1,0:T(8,128)(2,1)S(1)}, f32[8,64,256]{2,1,0:T(8,128)S(1)}, f32[8,512,256]{2,1,0:T(8,128)S(1)}, bf16[2,8,64,128]{3,2,1,0:T(8,128)(2,1)S(1)}) custom-call(bf16[2,128,128]{2,1,0:T(8,128)(2,1)} %bitcast.6, bf16[2,128,128]{2,1,0:T(8,128)(2,1)} %bitcast.7, bf16[16,128,512]{2,1,0:T(8,128)(2,1)} %bitcast.5, s32[10,2048]{1,0:T(8,128)} %rows_in.1, ...), custom_call_target="tpu_custom_call" | custom-call | tf_op jit(solution)/shard_map/pallas_call | solution.py:439
  33.9 2.3 %shard_map.56 = bf16[16,128,512]{2,1,0:T(8,128)(2,1)} custom-call(bf16[16,128,128]{2,1,0:T(8,128)(2,1)S(1)} %get-tuple-element.9.qbuf, f32[8,64,256]{2,1,0:T(8,128)S(1)} %get-tuple-element.10.sh, f32[8,512,256]{2,1,0:T(8,128)S(1)} %get-tuple-element.11.total, bf16[2,8,64,128]{3,2,1,0:T(8,128)(2,1)S(1)} %get-tuple-element.12.xst), custom_call_target="tpu_custom_call" | custom-call | tf_op jit(solution)/shard_map/pallas_call | solution.py:491

commit v4 on v3

--- a/solution.py
+++ b/solution.py
@@ -66,7 +66,7 @@
     barrier = pltpu.get_barrier_semaphore()
     next_x = [((x + d) % X * Z + z, head) for d in (1, X - 1)]
     next_z = [(ctx_z(d), head) for d in (1, Z - 1)]
-    partners = [(ctx, to) for to in (sib, up, down)] + next_z + next_x
+    partners = [(ctx, to) for to in (sib, up, down, far)] + next_z + next_x
     for to in partners:
         pl.semaphore_signal(barrier, 1, device_id=to, device_id_type=mesh_id)
     for cp in copies + v_copies:
@@ -77,25 +77,17 @@
         def g(i, a, b, to):
             return remote(a, b, gs_sem.at[n, i], gr_sem.at[n, i], head_to=to)
 
-        def part(h, half):
-            return buf.at[pl.ds(2 * h + half, 1)]
-
-        def whole(h):
+        def shard(h):
             return buf.at[pl.ds(2 * h, 2)]
 
-        first, second = src.at[pl.ds(0, 1)], src.at[pl.ds(1, 1)]
         return [
-            g(0, src, whole(head), sib),
-            g(1, first, part(head, 0), up),
-            g(2, second, part(head, 1), up),
-            g(3, second, part(head, 1), down),
-            g(4, first, part(head, 0), down),
-            g(5, part(down, 0), part(down, 0), up),
-            g(6, part(up, 1), part(up, 1), down),
-            g(7, whole(down), whole(down), sib),
-            g(8, whole(up), whole(up), sib),
-            g(9, part(far, 0), part(far, 0), sib),
-            g(10, part(far, 1), part(far, 1), sib),
+            g(0, src, shard(head), sib),
+            g(1, src, shard(head), up),
+            g(2, src, shard(head), down),
+            g(3, src, shard(head), far),
+            g(4, shard(down), shard(down), sib),
+            g(5, shard(up), shard(up), sib),
+            g(6, shard(far), shard(far), sib),
         ]
 
     def step(copies, *pairs):
@@ -105,7 +97,7 @@
 
     gk = gather(k_in, kbuf, 0)
     gq = gather(q_in, qbuf, 1)
-    for i in (1, 3, 2, 4, 0):
+    for i in (3, 1, 2, 0):
         gk[i].start()
     for to in next_z + next_x:
         pl.semaphore_signal(in_sem.at[0], 1, device_id=to, device_id_type=mesh_id)
@@ -137,8 +129,8 @@
             in_sem.at[1], 1, device_id=(ctx_z(d), head), device_id_type=mesh_id
         )
 
-    step(gk, (1, 5), (3, 6), (2, 7), (4, 8))
-    for i in (1, 3, 2, 4):
+    step(gk, (1, 4), (2, 5))
+    for i in (3, 1, 2):
         gq[i].start()
 
 
@@ -150,19 +142,18 @@
 
     copies[2].wait()
     states(head)
+    gk[0].wait_recv()
+    states(sib)
+    step(gk, (3, 6))
+    gq[0].start()
     states(down)
     states(up)
-    step(gk, (5, 9), (6, 10))
-    gq[0].start()
     states(far)
-    gk[0].wait_recv()
-    states(sib)
-    gk[7].wait_recv()
+    gk[4].wait_recv()
     states(down_s)
-    gk[8].wait_recv()
+    gk[5].wait_recv()
     states(up_s)
-    gk[9].wait_recv()
-    gk[10].wait_recv()
+    gk[6].wait_recv()
     states(far_s)
     pl.semaphore_wait(in_sem.at[1], 2)
 
@@ -189,10 +180,6 @@
     recv[z] = send[z]
 
     z_next = remote(send, zst.at[0], zs_sem.at[0, 0], zr_sem.at[0, 0], ctx_to=ctx_z(1))
-
-    @pl.when(z % 2 == 0)
-    def _():
-        z_next.start()
 
     causal = lax.broadcasted_iota(jnp.int32, (GROUP, GROUP), 0) >= lax.broadcasted_iota(
         jnp.int32, (GROUP, GROUP), 1
@@ -236,15 +223,18 @@
 
     copies[3].wait()
     near(head)
-    step(gq, (1, 5), (3, 6), (2, 7), (4, 8))
-    gq[0].wait_recv()
-    near(sib)
+
+    @pl.when(z % 2 == 0)
+    def _():
+        z_next.start()
+
+    step(gq, (1, 4), (2, 5))
 
     @pl.loop(0, 2)
     def _(e):
-        near((y + 3 + 2 * e) % Y * 2 + c)
-
-    step(gq, (5, 9), (6, 10))
+        near((y + 1 + 2 * e) % Y * 2 + c)
+
+    step(gq, (3, 6))
 
     for cp in a2a:
         cp.wait_recv()
@@ -268,42 +258,64 @@
     pair6[1] = s45.astype(BF16)
     half7[...] = s03.astype(BF16)
 
-    def t_copy(d):
-        to = (x + 1) % X * Z + z_at(d)
-        return remote(row_b, xst.at[0, z], bs_sem.at[0, d], br_sem.at[0, d], ctx_to=to)
-
-    def z_copy(level, d):
-        src = (None, pair6.at[z_at(d) // 4], half7)[level]
+    def t_copy(to):
+        ctx_to = (x + 1) % X * Z + to
+        return remote(row_b, xst.at[0, z], bs_sem.at[0, to], br_sem.at[0, z], ctx_to=ctx_to)
+
+    def z_copy(level, to):
+        src = (None, pair6.at[to // 4], half7)[level]
         return remote(
-            src, zst.at[level, z], zs_sem.at[level, d], zr_sem.at[level, d], ctx_to=ctx_z(d)
+            src, zst.at[level, z], zs_sem.at[level, to], zr_sem.at[level, z], ctx_to=x * Z + to
         )
 
-    order = (4, 3, 5, 2, 6, 1, 7)
-    for level in (2, 1):
-        for d in order:
-
-            @pl.when((z_at(d) >> level) % 2 == 1)
-            def _():
-                z_copy(level, d).start()
-
-    @pl.when(x % 2 == 0)
-    def _():
-        for d in order + (0,):
-            t_copy(d).start()
+    def z_send(level, to):
+        @pl.when(z != to)
+        def _():
+            z_copy(level, to).start()
+
+    low_z, high_z = range(4), range(4, 8)
+    even = x % 2 == 0
+
+    @pl.when(even)
+    def _():
+        for to in low_z:
+            t_copy(to).start()
+
+    for to in (2, 3):
+        z_send(1, to)
+
+    @pl.when(even)
+    def _():
+        for to in high_z:
+            t_copy(to).start()
+
+    for to in high_z:
+        z_send(2, to)
+    for to in (6, 7):
+        z_send(1, to)
 
     zst[1, z] = pair6[z // 4]
     zst[2, z] = half7[...]
 
-    gq[7].wait_recv()
-    gq[8].wait_recv()
-
-    @pl.loop(0, 2)
-    def _(e):
-        near((y + 3 + 2 * e) % Y * 2 + 1 - c)
-
-    def b_copy(d):
-        to = jnp.where(x == 1, ctx_z(d) + Z, ctx_z(d))
-        return remote(both, xst.at[1, z], bs_sem.at[1, d], br_sem.at[1, d], ctx_to=to)
+    gq[0].wait_recv()
+    near(far)
+    near(sib)
+
+    def b_copy(to):
+        ctx_to = jnp.where(x == 1, 2, x) * Z + to
+        return remote(both, xst.at[1, z], bs_sem.at[1, to], br_sem.at[1, z], ctx_to=ctx_to)
+
+    def b_send(to):
+        @pl.when(jnp.logical_or(x == 1, z != to))
+        def _():
+            b_copy(to).start()
+
+    def landed(sems, dst, sources):
+        for j in sources:
+
+            @pl.when(z != j)
+            def _():
+                remote(half7, dst.at[j], sems.at[j], sems.at[j]).wait_recv()
 
     def x_wait(s):
         remote(row_f, row_r.at[s], xs_sem.at[s], xr_sem.at[s]).wait_recv()
@@ -312,8 +324,6 @@
     def _():
         x_wait(0)
         both[...] = (row_r[0] + row_f[...]).astype(BF16)
-        for d in order + (0,):
-            b_copy(d).start()
 
     @pl.when(x == 3)
     def _():
@@ -322,19 +332,22 @@
         t = (row_r[0] + row_r[1]).astype(BF16)
         both[...] = t
         xst[1, z] = t
-        for d in order:
-            b_copy(d).start()
+
+    @pl.when(x % 2 == 1)
+    def _():
+        for to in range(Z):
+            b_send(to)
 
     @pl.when(x < 2)
     def _():
         xst[1] = jnp.zeros((8, CHUNK, 128), BF16)
 
-    gq[9].wait_recv()
-    gq[10].wait_recv()
-
-    @pl.loop(0, 2)
+    for i in (4, 5, 6):
+        gq[i].wait_recv()
+
+    @pl.loop(1, 4)
     def _(e):
-        near((y + 2) % Y * 2 + e)
+        near((y + e) % Y * 2 + 1 - c)
 
     def add_all(state, level):
         @pl.loop(0, 4)
@@ -347,27 +360,26 @@
         z_next.wait_recv()
         add_all(zst[0], 5)
 
-    for level in (2, 1):
+    for level in (1, 2):
+
         @pl.when((z >> level) % 2 == 1)
         def _():
-            for d in range(1, Z):
-                z_copy(level, d).wait_recv()
+            landed(zr_sem.at[level], zst.at[level], range(Z))
             add_all(zst[level], 5 + level)
 
     @pl.when(x % 2 == 1)
     def _():
-        for d in range(Z):
-            t_copy(d).wait_recv()
+        landed(br_sem.at[0], xst.at[0], range(Z))
+        remote(half7, xst.at[0, z], br_sem.at[0, z], br_sem.at[0, z]).wait_recv()
         add_all(xst[0], 8)
 
     @pl.when(x >= 2)
     def _():
-        for d in range(1, Z):
-            b_copy(d).wait_recv()
+        landed(br_sem.at[1], xst.at[1], range(Z))
 
     @pl.when(x == 2)
     def _():
-        b_copy(0).wait_recv()
+        remote(half7, xst.at[1, z], br_sem.at[1, z], br_sem.at[1, z]).wait_recv()
 
     for cp in gk + gq + a2a:
         cp.wait_send()
@@ -382,32 +394,31 @@
         def _():
             x_copy(to).wait_send()
 
-    for level in (2, 1):
-        for d in range(1, Z):
-
-            @pl.when((z_at(d) >> level) % 2 == 1)
+    for level, targets in ((2, high_z), (1, (2, 3, 6, 7))):
+        for to in targets:
+
+            @pl.when(z != to)
             def _():
-                z_copy(level, d).wait_send()
-
-    @pl.when(x % 2 == 0)
-    def _():
-        for d in range(Z):
-            t_copy(d).wait_send()
+                z_copy(level, to).wait_send()
+
+    @pl.when(even)
+    def _():
+        for to in range(Z):
+            t_copy(to).wait_send()
 
     @pl.when(x % 2 == 1)
     def _():
-        for d in range(1, Z):
-            b_copy(d).wait_send()
-
-    @pl.when(x == 1)
-    def _():
-        b_copy(0).wait_send()
+        for to in range(Z):
+
+            @pl.when(jnp.logical_or(x == 1, z != to))
+            def _():
+                b_copy(to).wait_send()
 
 
 def finish(qbuf, sh, total, xst, out, obuf, o_sem):
-    def o_copy(m):
-        g = pl.ds(4 * m, 4)
-        return pltpu.make_async_copy(obuf.at[g], out.at[g], o_sem.at[m])
+    def o_copy(i):
+        g = pl.ds(2 * i, 2)
+        return pltpu.make_async_copy(obuf.at[g], out.at[g], o_sem.at[i])
 
     @pl.loop(0, 4)
     def _(m):
@@ -418,10 +429,10 @@
                 lane = 16 * h + 9
                 t = total[i, rows, :] + f[rows] * sh[i, lane : lane + 1, :]
                 obuf[pl.ds(2 * i, 2), :, rows] = t.astype(BF16).T.reshape(2, GROUP, GROUP)
-        o_copy(m).start()
-
-    for m in range(4):
-        o_copy(m).wait()
+            o_copy(i).start()
+
+    for i in range(8):
+        o_copy(i).wait()
 
 
 def local(queries, keys, values, tier_weight_rows, level_table):
@@ -463,8 +474,8 @@
             vm((3, 8, CHUNK, 128), BF16),
             DMA((4,)),
             DMA((8,)),
-            DMA((2, 11)),
-            DMA((2, 11)),
+            DMA((2, 7)),
+            DMA((2, 7)),
             DMA((8,)),
             DMA((8,)),
             DMA((3, 8)),
@@ -493,7 +504,7 @@
         out_shape=jax.ShapeDtypeStruct((groups, GROUP, columns), BF16),
         in_specs=in_vmem,
         out_specs=anywhere,
-        scratch_shapes=[vm((groups, GROUP, columns), BF16), DMA((4,))],
+        scratch_shapes=[vm((groups, GROUP, columns), BF16), DMA((8,))],
         compiler_params=pltpu.CompilerParams(vmem_limit_bytes=12 * 2**20),
     )(*parts)
     return out.reshape(tokens, columns)

time: 36.3 us -> 33.2 us (0.915)
  Pallas kernels: 36.2 us -> 33.1 us
    pallas_call x1, Pallas kernels: 33.9 us -> 30.6 us  [local(): pl.pallas_call(kernel, out_shape=kept, in_specs=[pl.BlockSpec(memory_spac...]
where the time goes in v4:
time: 33.2 us; the launch traced here: 33.1 us
  Pallas kernels  33.1 us (100%)
    pallas_call x1, Pallas kernels, local(): pl.pallas_call(kernel, out_shape=kept, in_specs=[pl.BlockSpec(memory_spac...  30.6 us
    pallas_call x1, Pallas kernels, local(): pl.pallas_call(finish, out_shape=jax.ShapeDtypeStruct((groups, GROUP, col...  2.41 us

profile of v4, /device:TPU:2, one launch (start us, length us, event | category | flops | bytes accessed | tf_op | source)
XLA Modules:
  0.0 33.1 jit_solution(1278969235406320022)
XLA Ops:
  0.0 30.6 %shard_map.55 = (bf16[16,128,128]{2,1,0:T(8,128)(2,1)S(1)}, f32[8,64,256]{2,1,0:T(8,128)S(1)}, f32[8,512,256]{2,1,0:T(8,128)S(1)}, bf16[2,8,64,128]{3,2,1,0:T(8,128)(2,1)S(1)}) custom-call(bf16[2,128,128]{2,1,0:T(8,128)(2,1)} %bitcast.6, bf16[2,128,128]{2,1,0:T(8,128)(2,1)} %bitcast.7, bf16[16,128,512]{2,1,0:T(8,128)(2,1)} %bitcast.5, s32[10,2048]{1,0:T(8,128)} %rows_in.1, ...), custom_call_target="tpu_custom_call" | custom-call | tf_op jit(solution)/shard_map/pallas_call | solution.py:450
  30.7 2.4 %shard_map.56 = bf16[16,128,512]{2,1,0:T(8,128)(2,1)} custom-call(bf16[16,128,128]{2,1,0:T(8,128)(2,1)S(1)} %get-tuple-element.9.qbuf, f32[8,64,256]{2,1,0:T(8,128)S(1)} %get-tuple-element.10.sh, f32[8,512,256]{2,1,0:T(8,128)S(1)} %get-tuple-element.11.total, bf16[2,8,64,128]{3,2,1,0:T(8,128)(2,1)S(1)} %get-tuple-element.12.xst), custom_call_target="tpu_custom_call" | custom-call | tf_op jit(solution)/shard_map/pallas_call | solution.py:502

commit v5 on v4

--- a/solution.py
+++ b/solution.py
@@ -273,26 +273,26 @@
         def _():
             z_copy(level, to).start()
 
-    low_z, high_z = range(4), range(4, 8)
+    high_z = range(4, 8)
     even = x % 2 == 0
 
-    @pl.when(even)
-    def _():
-        for to in low_z:
-            t_copy(to).start()
-
-    for to in (2, 3):
+    def t_send(*targets):
+        @pl.when(even)
+        def _():
+            for to in targets:
+                t_copy(to).start()
+
+    t_send(0, 1)
+    z_send(1, 2)
+    z_send(1, 3)
+    t_send(2, 3)
+    z_send(2, 4)
+    z_send(2, 5)
+    t_send(4, 5)
+    for to in (6, 7):
+        z_send(2, to)
         z_send(1, to)
-
-    @pl.when(even)
-    def _():
-        for to in high_z:
-            t_copy(to).start()
-
-    for to in high_z:
-        z_send(2, to)
-    for to in (6, 7):
-        z_send(1, to)
+    t_send(6, 7)
 
     zst[1, z] = pair6[z // 4]
     zst[2, z] = half7[...]
@@ -300,6 +300,12 @@
     gq[0].wait_recv()
     near(far)
     near(sib)
+    gq[4].wait_recv()
+    gq[5].wait_recv()
+
+    @pl.loop(0, 2)
+    def _(e):
+        near((y + 1 + 2 * e) % Y * 2 + 1 - c)
 
     def b_copy(to):
         ctx_to = jnp.where(x == 1, 2, x) * Z + to
@@ -338,16 +344,8 @@
         for to in range(Z):
             b_send(to)
 
-    @pl.when(x < 2)
-    def _():
-        xst[1] = jnp.zeros((8, CHUNK, 128), BF16)
-
-    for i in (4, 5, 6):
-        gq[i].wait_recv()
-
-    @pl.loop(1, 4)
-    def _(e):
-        near((y + e) % Y * 2 + 1 - c)
+    gq[6].wait_recv()
+    near(far_s)
 
     def add_all(state, level):
         @pl.loop(0, 4)
@@ -371,6 +369,9 @@
     def _():
         landed(br_sem.at[0], xst.at[0], range(Z))
         remote(half7, xst.at[0, z], br_sem.at[0, z], br_sem.at[0, z]).wait_recv()
+
+    @pl.when(x == 3)
+    def _():
         add_all(xst[0], 8)
 
     @pl.when(x >= 2)
@@ -420,16 +421,26 @@
         g = pl.ds(2 * i, 2)
         return pltpu.make_async_copy(obuf.at[g], out.at[g], o_sem.at[i])
 
-    @pl.loop(0, 4)
-    def _(m):
-        for i in (2 * m, 2 * m + 1):
-            f = nt(xst[1].reshape(512, 128), qbuf[pl.ds(2 * i, 2)].reshape(256, 128))
-            for h in range(4):
-                rows = slice(h * GROUP, (h + 1) * GROUP)
-                lane = 16 * h + 9
-                t = total[i, rows, :] + f[rows] * sh[i, lane : lane + 1, :]
-                obuf[pl.ds(2 * i, 2), :, rows] = t.astype(BF16).T.reshape(2, GROUP, GROUP)
-            o_copy(i).start()
+    def run(level):
+        @pl.loop(0, 4)
+        def _(m):
+            for i in (2 * m, 2 * m + 1):
+                if level:
+                    state = xst[level - 8].reshape(512, 128)
+                    f = nt(state, qbuf[pl.ds(2 * i, 2)].reshape(256, 128))
+                for h in range(4):
+                    rows = slice(h * GROUP, (h + 1) * GROUP)
+                    t = total[i, rows, :]
+                    if level:
+                        lane = 16 * h + level
+                        t += f[rows] * sh[i, lane : lane + 1, :]
+                    obuf[pl.ds(2 * i, 2), :, rows] = t.astype(BF16).T.reshape(2, GROUP, GROUP)
+                o_copy(i).start()
+
+    x = lax.axis_index("ctx") // Z
+    pl.when(x >= 2)(lambda: run(9))
+    pl.when(x == 1)(lambda: run(8))
+    pl.when(x == 0)(lambda: run(None))
 
     for i in range(8):
         o_copy(i).wait()

time: 33.2 us -> 32.2 us (0.970)
  the two profiles are of different devices: /device:TPU:2 before, /device:TPU:6 now
where the time goes in v5:
time: 32.2 us; the launch traced here: 31.6 us
  Pallas kernels  31.6 us (98%)
    pallas_call x1, Pallas kernels, local(): pl.pallas_call(kernel, out_shape=kept, in_specs=[pl.BlockSpec(memory_spac...  29.1 us
    pallas_call x1, Pallas kernels, local(): pl.pallas_call(finish, out_shape=jax.ShapeDtypeStruct((groups, GROUP, col...  2.43 us

profile of v5, /device:TPU:6, one launch (start us, length us, event | category | flops | bytes accessed | tf_op | source)
XLA Modules:
  0.0 31.6 jit_solution(17144205366261623122)
XLA Ops:
  0.0 29.1 %shard_map.55 = (bf16[16,128,128]{2,1,0:T(8,128)(2,1)S(1)}, f32[8,64,256]{2,1,0:T(8,128)S(1)}, f32[8,512,256]{2,1,0:T(8,128)S(1)}, bf16[2,8,64,128]{3,2,1,0:T(8,128)(2,1)S(1)}) custom-call(bf16[2,128,128]{2,1,0:T(8,128)(2,1)} %bitcast.6, bf16[2,128,128]{2,1,0:T(8,128)(2,1)} %bitcast.7, bf16[16,128,512]{2,1,0:T(8,128)(2,1)} %bitcast.5, s32[10,2048]{1,0:T(8,128)} %rows_in.1, ...), custom_call_target="tpu_custom_call" | custom-call | tf_op jit(solution)/shard_map/pallas_call | solution.py:461
  29.1 2.4 %shard_map.56 = bf16[16,128,512]{2,1,0:T(8,128)(2,1)} custom-call(bf16[16,128,128]{2,1,0:T(8,128)(2,1)S(1)} %get-tuple-element.9.qbuf, f32[8,64,256]{2,1,0:T(8,128)S(1)} %get-tuple-element.10.sh, f32[8,512,256]{2,1,0:T(8,128)S(1)} %get-tuple-element.11.total, bf16[2,8,64,128]{3,2,1,0:T(8,128)(2,1)S(1)} %get-tuple-element.12.xst), custom_call_target="tpu_custom_call" | custom-call | tf_op jit(solution)/shard_map/pallas_call | solution.py:513

commit v6 on v5

--- a/solution.py
+++ b/solution.py
@@ -28,7 +28,7 @@
     kbuf, vbuf, vt, rows, table, pairs, lev1, lev2, lev3, lev4,
     send, recv, pair6, half7, row_f, row_b, row_r, both, zst,
     loc_sem, v_sem, gs_sem, gr_sem, as_sem, ar_sem, zs_sem, zr_sem,
-    xs_sem, xr_sem, bs_sem, br_sem, in_sem,
+    xs_sem, xr_sem, bs_sem, br_sem, ps_sem, in_sem,
 ):
     ctx = lax.axis_index("ctx")
     head = lax.axis_index("head")
@@ -181,6 +181,10 @@
 
     z_next = remote(send, zst.at[0], zs_sem.at[0, 0], zr_sem.at[0, 0], ctx_to=ctx_z(1))
 
+    @pl.when(z % 2 == 0)
+    def _():
+        z_next.start()
+
     causal = lax.broadcasted_iota(jnp.int32, (GROUP, GROUP), 0) >= lax.broadcasted_iota(
         jnp.int32, (GROUP, GROUP), 1
     )
@@ -224,10 +228,6 @@
     copies[3].wait()
     near(head)
 
-    @pl.when(z % 2 == 0)
-    def _():
-        z_next.start()
-
     step(gq, (1, 4), (2, 5))
 
     @pl.loop(0, 2)
@@ -268,10 +268,22 @@
             src, zst.at[level, z], zs_sem.at[level, to], zr_sem.at[level, z], ctx_to=x * Z + to
         )
 
+    def direct(level, to):
+        ok = z != to
+        if level == 2:
+            ok = jnp.logical_and(ok, z >= 4)
+        return ok
+
     def z_send(level, to):
-        @pl.when(z != to)
+        @pl.when(direct(level, to))
         def _():
             z_copy(level, to).start()
+
+    mate = jnp.maximum(z - 4, 0)
+
+    def pass_on(to):
+        slot = zst.at[2, mate]
+        return remote(slot, slot, ps_sem.at[to - 4], zr_sem.at[2, mate], ctx_to=x * Z + to)
 
     high_z = range(4, 8)
     even = x % 2 == 0
@@ -281,6 +293,10 @@
         def _():
             for to in targets:
                 t_copy(to).start()
+
+    @pl.when(z < 4)
+    def _():
+        z_copy(2, z + 4).start()
 
     t_send(0, 1)
     z_send(1, 2)
@@ -301,11 +317,7 @@
     near(far)
     near(sib)
     gq[4].wait_recv()
-    gq[5].wait_recv()
-
-    @pl.loop(0, 2)
-    def _(e):
-        near((y + 1 + 2 * e) % Y * 2 + 1 - c)
+    near(down_s)
 
     def b_copy(to):
         ctx_to = jnp.where(x == 1, 2, x) * Z + to
@@ -316,10 +328,13 @@
         def _():
             b_copy(to).start()
 
-    def landed(sems, dst, sources):
+    def landed(sems, dst, sources, had=None):
         for j in sources:
-
-            @pl.when(z != j)
+            there = z == j
+            if had is not None:
+                there = jnp.logical_or(there, had == j)
+
+            @pl.when(jnp.logical_not(there))
             def _():
                 remote(half7, dst.at[j], sems.at[j], sems.at[j]).wait_recv()
 
@@ -344,8 +359,21 @@
         for to in range(Z):
             b_send(to)
 
+    gq[5].wait_recv()
     gq[6].wait_recv()
-    near(far_s)
+
+    @pl.loop(1, 3)
+    def _(e):
+        near((y + e) % Y * 2 + 1 - c)
+
+    @pl.when(z >= 4)
+    def _():
+        remote(half7, zst.at[2, mate], zr_sem.at[2, mate], zr_sem.at[2, mate]).wait_recv()
+        for to in high_z:
+
+            @pl.when(z != to)
+            def _():
+                pass_on(to).start()
 
     def add_all(state, level):
         @pl.loop(0, 4)
@@ -362,7 +390,7 @@
 
         @pl.when((z >> level) % 2 == 1)
         def _():
-            landed(zr_sem.at[level], zst.at[level], range(Z))
+            landed(zr_sem.at[level], zst.at[level], range(Z), mate if level == 2 else None)
             add_all(zst[level], 5 + level)
 
     @pl.when(x % 2 == 1)
@@ -398,9 +426,21 @@
     for level, targets in ((2, high_z), (1, (2, 3, 6, 7))):
         for to in targets:
 
+            @pl.when(direct(level, to))
+            def _():
+                z_copy(level, to).wait_send()
+
+    @pl.when(z < 4)
+    def _():
+        z_copy(2, z + 4).wait_send()
+
+    @pl.when(z >= 4)
+    def _():
+        for to in high_z:
+
             @pl.when(z != to)
             def _():
-                z_copy(level, to).wait_send()
+                pass_on(to).wait_send()
 
     @pl.when(even)
     def _():
@@ -495,6 +535,7 @@
             DMA((2,)),
             DMA((2, 8)),
             DMA((2, 8)),
+            DMA((4,)),
             pltpu.SemaphoreType.REGULAR((2,)),
         ],
         compiler_params=pltpu.CompilerParams(

time: 32.2 us -> 31.9 us (level); the launches traced: 31.6 us -> 31.8 us
  no operation moved by 1% of the time
where the time goes in v6:
time: 31.9 us; the launch traced here: 31.8 us
  Pallas kernels  31.8 us (100%)
    pallas_call x1, Pallas kernels, local(): pl.pallas_call(kernel, out_shape=kept, in_specs=[pl.BlockSpec(memory_spac...  29.4 us
    pallas_call x1, Pallas kernels, local(): pl.pallas_call(finish, out_shape=jax.ShapeDtypeStruct((groups, GROUP, col...  2.43 us

profile of v6, /device:TPU:6, one launch (start us, length us, event | category | flops | bytes accessed | tf_op | source)
XLA Modules:
  0.0 31.8 jit_solution(9967719050076939397)
XLA Ops:
  0.0 29.4 %shard_map.55 = (bf16[16,128,128]{2,1,0:T(8,128)(2,1)S(1)}, f32[8,64,256]{2,1,0:T(8,128)S(1)}, f32[8,512,256]{2,1,0:T(8,128)S(1)}, bf16[2,8,64,128]{3,2,1,0:T(8,128)(2,1)S(1)}) custom-call(bf16[2,128,128]{2,1,0:T(8,128)(2,1)} %bitcast.6, bf16[2,128,128]{2,1,0:T(8,128)(2,1)} %bitcast.7, bf16[16,128,512]{2,1,0:T(8,128)(2,1)} %bitcast.5, s32[10,2048]{1,0:T(8,128)} %rows_in.1, ...), custom_call_target="tpu_custom_call" | custom-call | tf_op jit(solution)/shard_map/pallas_call | solution.py:501
  29.4 2.4 %shard_map.56 = bf16[16,128,512]{2,1,0:T(8,128)(2,1)} custom-call(bf16[16,128,128]{2,1,0:T(8,128)(2,1)S(1)} %get-tuple-element.9.qbuf, f32[8,64,256]{2,1,0:T(8,128)S(1)} %get-tuple-element.10.sh, f32[8,512,256]{2,1,0:T(8,128)S(1)} %get-tuple-element.11.total, bf16[2,8,64,128]{3,2,1,0:T(8,128)(2,1)S(1)} %get-tuple-element.12.xst), custom_call_target="tpu_custom_call" | custom-call | tf_op jit(solution)/shard_map/pallas_call | solution.py:554

commit v7 on v6

--- a/solution.py
+++ b/solution.py
@@ -243,9 +243,10 @@
     s03 = s01 + s23
     row = s03 + s45 + s67
     row_f[...] = row
+    row_b[...] = row.astype(BF16)
 
     def x_copy(to):
-        return remote(row_f, row_r.at[x], xs_sem.at[to], xr_sem.at[x], ctx_to=to * Z + z)
+        return remote(row_b, row_r.at[x], xs_sem.at[to], xr_sem.at[x], ctx_to=to * Z + z)
 
     for to, sender in ((3, x < 2), (1, x == 0)):
 
@@ -253,7 +254,6 @@
         def _():
             x_copy(to).start()
 
-    row_b[...] = row.astype(BF16)
     pair6[0] = s01.astype(BF16)
     pair6[1] = s45.astype(BF16)
     half7[...] = s03.astype(BF16)
@@ -339,18 +339,18 @@
                 remote(half7, dst.at[j], sems.at[j], sems.at[j]).wait_recv()
 
     def x_wait(s):
-        remote(row_f, row_r.at[s], xs_sem.at[s], xr_sem.at[s]).wait_recv()
+        remote(row_b, row_r.at[s], xs_sem.at[s], xr_sem.at[s]).wait_recv()
 
     @pl.when(x == 1)
     def _():
         x_wait(0)
-        both[...] = (row_r[0] + row_f[...]).astype(BF16)
+        both[...] = (row_r[0].astype(F32) + row_f[...]).astype(BF16)
 
     @pl.when(x == 3)
     def _():
         x_wait(0)
         x_wait(1)
-        t = (row_r[0] + row_r[1]).astype(BF16)
+        t = (row_r[0].astype(F32) + row_r[1].astype(F32)).astype(BF16)
         both[...] = t
         xst[1, z] = t
 
@@ -520,7 +520,7 @@
             vm((CHUNK, 128), BF16),
             vm((CHUNK, 128), F32),
             vm((CHUNK, 128), BF16),
-            vm((2, CHUNK, 128), F32),
+            vm((2, CHUNK, 128), BF16),
             vm((CHUNK, 128), BF16),
             vm((3, 8, CHUNK, 128), BF16),
             DMA((4,)),

time: 31.9 us -> 32 us (level)
  no operation moved by 1% of the time
where the time goes in v7:
time: 32 us; the launch traced here: 31.9 us
  Pallas kernels  31.9 us (100%)
    pallas_call x1, Pallas kernels, local(): pl.pallas_call(kernel, out_shape=kept, in_specs=[pl.BlockSpec(memory_spac...  29.4 us
    pallas_call x1, Pallas kernels, local(): pl.pallas_call(finish, out_shape=jax.ShapeDtypeStruct((groups, GROUP, col...  2.43 us

profile of v7, /device:TPU:6, one launch (start us, length us, event | category | flops | bytes accessed | tf_op | source)
XLA Modules:
  0.0 31.9 jit_solution(13120562094795687710)
XLA Ops:
  0.0 29.4 %shard_map.55 = (bf16[16,128,128]{2,1,0:T(8,128)(2,1)S(1)}, f32[8,64,256]{2,1,0:T(8,128)S(1)}, f32[8,512,256]{2,1,0:T(8,128)S(1)}, bf16[2,8,64,128]{3,2,1,0:T(8,128)(2,1)S(1)}) custom-call(bf16[2,128,128]{2,1,0:T(8,128)(2,1)} %bitcast.6, bf16[2,128,128]{2,1,0:T(8,128)(2,1)} %bitcast.7, bf16[16,128,512]{2,1,0:T(8,128)(2,1)} %bitcast.5, s32[10,2048]{1,0:T(8,128)} %rows_in.1, ...), custom_call_target="tpu_custom_call" | custom-call | tf_op jit(solution)/shard_map/pallas_call | solution.py:501
  29.5 2.4 %shard_map.56 = bf16[16,128,512]{2,1,0:T(8,128)(2,1)} custom-call(bf16[16,128,128]{2,1,0:T(8,128)(2,1)S(1)} %get-tuple-element.9.qbuf, f32[8,64,256]{2,1,0:T(8,128)S(1)} %get-tuple-element.10.sh, f32[8,512,256]{2,1,0:T(8,128)S(1)} %get-tuple-element.11.total, bf16[2,8,64,128]{3,2,1,0:T(8,128)(2,1)S(1)} %get-tuple-element.12.xst), custom_call_target="tpu_custom_call" | custom-call | tf_op jit(solution)/shard_map/pallas_call | solution.py:554

commit v8 on v6

--- a/solution.py
+++ b/solution.py
@@ -462,9 +462,9 @@
         return pltpu.make_async_copy(obuf.at[g], out.at[g], o_sem.at[i])
 
     def run(level):
-        @pl.loop(0, 4)
+        @pl.loop(0, 2)
         def _(m):
-            for i in (2 * m, 2 * m + 1):
+            for i in (4 * m, 4 * m + 1, 4 * m + 2, 4 * m + 3):
                 if level:
                     state = xst[level - 8].reshape(512, 128)
                     f = nt(state, qbuf[pl.ds(2 * i, 2)].reshape(256, 128))

time: 31.9 us -> 31.5 us (0.987)
  Pallas kernels: 31.8 us -> 31.4 us
    pallas_call x1, Pallas kernels: 2.43 us -> 1.96 us  [local(): pl.pallas_call(finish, out_shape=jax.ShapeDtypeStruct((groups, GROUP, col...]
where the time goes in v8:
time: 31.5 us; the launch traced here: 31.4 us
  Pallas kernels  31.4 us (100%)
    pallas_call x1, Pallas kernels, local(): pl.pallas_call(kernel, out_shape=kept, in_specs=[pl.BlockSpec(memory_spac...  29.4 us
    pallas_call x1, Pallas kernels, local(): pl.pallas_call(finish, out_shape=jax.ShapeDtypeStruct((groups, GROUP, col...  1.96 us

profile of v8, /device:TPU:6, one launch (start us, length us, event | category | flops | bytes accessed | tf_op | source)
XLA Modules:
  0.0 31.4 jit_solution(241185561814680769)
XLA Ops:
  0.0 29.4 %shard_map.55 = (bf16[16,128,128]{2,1,0:T(8,128)(2,1)S(1)}, f32[8,64,256]{2,1,0:T(8,128)S(1)}, f32[8,512,256]{2,1,0:T(8,128)S(1)}, bf16[2,8,64,128]{3,2,1,0:T(8,128)(2,1)S(1)}) custom-call(bf16[2,128,128]{2,1,0:T(8,128)(2,1)} %bitcast.6, bf16[2,128,128]{2,1,0:T(8,128)(2,1)} %bitcast.7, bf16[16,128,512]{2,1,0:T(8,128)(2,1)} %bitcast.5, s32[10,2048]{1,0:T(8,128)} %rows_in.1, ...), custom_call_target="tpu_custom_call" | custom-call | tf_op jit(solution)/shard_map/pallas_call | solution.py:501
  29.4 2.0 %shard_map.56 = bf16[16,128,512]{2,1,0:T(8,128)(2,1)} custom-call(bf16[16,128,128]{2,1,0:T(8,128)(2,1)S(1)} %get-tuple-element.9.qbuf, f32[8,64,256]{2,1,0:T(8,128)S(1)} %get-tuple-element.10.sh, f32[8,512,256]{2,1,0:T(8,128)S(1)} %get-tuple-element.11.total, bf16[2,8,64,128]{3,2,1,0:T(8,128)(2,1)S(1)} %get-tuple-element.12.xst), custom_call_target="tpu_custom_call" | custom-call | tf_op jit(solution)/shard_map/pallas_call | solution.py:554
